TPU v7x, 32 devices: a whole 2x2x4 slice. The times are simulated.
32 devices in a mesh: wide: 16 (over z, x, core), narrow: 2 (over y).
Axes of the slice: x: 2, y: 2, z: 4, core: 2. Of those that a mesh axis runs over, the one named last changes fastest.
Arguments:
- tokens: bfloat16 [16384, 768], P(('wide', 'narrow')), may hold values from -6 to 6
- token_marks: int32 [16384], P(('wide', 'narrow')), may hold values 0 or 1
- crop_lengths: int32 [256], P('wide'), may hold values from 0 to 576, as said below
- bucket_ids: int32 [256], P('wide'), may hold values from 0 to 3
- mask_token: bfloat16 [768], replicated, may hold values from -5 to 5
- norm1_gain: bfloat16 [768], replicated, may hold values from 0.099609375 to 1.8984375
- norm1_bias: bfloat16 [768], replicated, may hold values from -3 to 3
- w_qkv: bfloat16 [3, 768, 768], P(None, None, 'narrow'), may hold values from -0.21875 to 0.21875
- qv_bias: bfloat16 [2, 768], P(None, 'narrow'), may hold values from -3 to 3
- w_proj: bfloat16 [768, 768], P('narrow'), may hold values from -1.75 to 1.75
- proj_bias: bfloat16 [768], replicated, may hold values from -3 to 3
- scale_attn: bfloat16 [768], replicated, may hold values from 0.5 to 1.5
- norm2_gain: bfloat16 [768], replicated, may hold values from 0.099609375 to 1.8984375
- norm2_bias: bfloat16 [768], replicated, may hold values from -3 to 3
- w_fc1: bfloat16 [768, 3072], P(None, 'narrow'), may hold values from -0.21875 to 0.21875
- fc1_bias: bfloat16 [3072], P('narrow'), may hold values from -3 to 3
- w_fc2: bfloat16 [3072, 768], P('narrow'), may hold values from -0.109375 to 0.109375
- fc2_bias: bfloat16 [768], replicated, may hold values from -3 to 3
- scale_mlp: bfloat16 [768], replicated, may hold values from 0.5 to 1.5
- cotangent: bfloat16 [16384, 768], P(('wide', 'narrow')), may hold values from -6 to 6
Outputs:
- output: bfloat16 [16384, 768], P(('wide', 'narrow'))
- grad_tokens: float32 [16384, 768], P(('wide', 'narrow'))
- grad_mask_token: float32 [768], replicated
- grad_norm1_gain: float32 [768], replicated
- grad_norm1_bias: float32 [768], replicated
- grad_qkv: float32 [3, 768, 768], P(None, None, 'narrow')
- grad_qv_bias: float32 [2, 768], P(None, 'narrow')
- grad_proj: float32 [768, 768], P('narrow')
- grad_proj_bias: float32 [768], replicated
- grad_scale_attn: float32 [768], replicated
- grad_norm2_gain: float32 [768], replicated
- grad_norm2_bias: float32 [768], replicated
- grad_fc1: float32 [768, 3072], P(None, 'narrow')
- grad_fc1_bias: float32 [3072], P('narrow')
- grad_fc2: float32 [3072, 768], P('narrow')
- grad_fc2_bias: float32 [768], replicated
- grad_scale_mlp: float32 [768], replicated
Inputs may be any that keep to these rules, and one draw needn't show every extreme that they name: `crop_lengths`: length 0 marks an empty slot. The nonempty slots of a buffer come first, and their padded rows together fill at most 1024; some buffer is filled to exactly 1024 rows. A nonempty crop has more than 48 rows, and its bucket is the smallest of 64, 144, 256, 576 that holds it.
All inputs are finite; a program needn't handle non-finite values. No bound on the sum of `token_marks` on one device may be relied on, other than what follows from the above.
Results may differ from a plain program's by a relative error of at most 0.017.
Values may be sent and summed in bfloat16 or wider, within the bound.
No kernel may reach another device: no remote copies, remote signals or barrier semaphores. Data moves between devices by JAX's collectives and lax.ppermute only.
A program may use at most 128 MiB of HBM per device.

v0:
```python
from functools import partial

import jax
import jax.numpy as jnp
from jax import lax
from jax.experimental import pallas as pl
from jax.experimental.pallas import tpu as pltpu
from jax.sharding import PartitionSpec as P

HEAD_DIM = 64
B0 = 64
B1 = 144
B2 = 256
B3 = 576

epsilon = 1e-06
masked_score = -1e30
F32 = jnp.float32
BF16 = jnp.bfloat16
WINDOW = 256
BIG_ROWS = 128
SWAP = ((0, 1), (1, 0))


def nn(a, b):
    return lax.dot_general(a, b, (((1,), (0,)), ((), ())), preferred_element_type=F32)


def nt(a, b):
    return lax.dot_general(a, b, (((1,), (1,)), ((), ())), preferred_element_type=F32)


def tn(a, b):
    return lax.dot_general(a, b, (((0,), (0,)), ((), ())), preferred_element_type=F32)


def normed_of(rows_in):
    width = rows_in.shape[-1]
    mean = jnp.sum(rows_in, axis=-1, keepdims=True) * (1.0 / width)
    centered = rows_in - mean
    variance = jnp.sum(centered * centered, axis=-1, keepdims=True) * (1.0 / width)
    inverse = lax.rsqrt(variance + epsilon)
    return centered * inverse, inverse


def norm_back(grad, gain, normal, inverse):
    width = grad.shape[-1]
    g = grad * gain
    mean_g = jnp.sum(g, axis=-1, keepdims=True) * (1.0 / width)
    mean_gn = jnp.sum(g * normal, axis=-1, keepdims=True) * (1.0 / width)
    return (g - mean_g - normal * mean_gn) * inverse


def estimate(micros):
    return pl.CostEstimate(flops=int(micros * 1e9), bytes_accessed=1000, transcendentals=0)


def call(kernel, out_shape, args, micros, name, scratch=(), scalars=0):
    spec = pltpu.PrefetchScalarGridSpec(
        num_scalar_prefetch=scalars,
        grid=(),
        in_specs=[pl.BlockSpec(memory_space=pltpu.VMEM)] * (len(args) - scalars),
        out_specs=jax.tree.map(lambda s: pl.BlockSpec(memory_space=pltpu.VMEM), out_shape),
        scratch_shapes=list(scratch),
    )
    return pl.pallas_call(
        kernel,
        out_shape=out_shape,
        grid_spec=spec,
        compiler_params=pltpu.CompilerParams(vmem_limit_bytes=22 * 1024 * 1024),
        cost_estimate=estimate(micros),
        name=name,
    )(*args)


def shape(dims, kind=BF16):
    return jax.ShapeDtypeStruct(tuple(dims), kind)


def row_of(ref, k):
    return ref[k : k + 1, :].astype(F32)


def over_rows(total, body, carry=0):
    def step(i, carry):
        result = body(pl.ds(pl.multiple_of(i * WINDOW, WINDOW), WINDOW), carry)
        return carry if result is None else result

    return lax.fori_loop(0, total // WINDOW, step, carry)


def project_rows(tokens_ref, mark_ref, vec_ref, w_ref, normed_ref, x_ref, store):
    local = w_ref.shape[2]
    count = x_ref.shape[0]
    for first in range(0, count, count):
        rows = pl.ds(first, count)
        x = jnp.where(mark_ref[rows, :] > 0.5, vec_ref[8:9, :], tokens_ref[rows, :])
        x_ref[rows, :] = x
        normal, inverse = normed_of(x.astype(F32))
        normed = (normal * row_of(vec_ref, 0) + row_of(vec_ref, 1)).astype(BF16)
        normed_ref[rows, :] = normed
        for c in range(3):
            part = nn(normed, w_ref[c])
            if c != 1:
                start = 0 if c == 0 else local
                part = part + vec_ref[9:10, start : start + local].astype(F32)
            part = part.astype(BF16)
            if c == 0:
                part = part * 0.125
            for p in range(local // 128):
                store(c, p, first, part[:, p * 128 : (p + 1) * 128])


def qkv_kernel(tokens_ref, mark_ref, vec_ref, w_ref, normed_ref, qkv_ref, x_ref):
    def store(c, p, first, value):
        qkv_ref[c, p, pl.ds(first, value.shape[0]), :] = value

    project_rows(tokens_ref, mark_ref, vec_ref, w_ref, normed_ref, x_ref, store)


def slot_rows(meta, slot):
    bucket = meta[32 + slot]
    rows = jnp.where(bucket == 0, B0, jnp.where(bucket == 1, B1, jnp.where(bucket == 2, B2, B3)))
    return jnp.where(meta[slot] > 0, rows, 0)


def walk_groups(meta, slots, small, big):
    def more(state):
        slot, first = state
        return jnp.logical_and(slot < slots, meta[slot] > 0)

    def step(state):
        slot, first = state
        first = pl.multiple_of(first, 16)
        rows = slot_rows(meta, slot)

        def take_big():
            big(first, meta[slot])
            return slot + 1, first + B3

        def take_small():
            starts, ends, lasts = [jnp.int32(0)], [rows], [meta[slot]]
            going, end, count = jnp.bool_(True), rows, jnp.int32(1)
            for k in range(1, 4):
                size = slot_rows(meta, slot + k)
                going = going & (slot + k < slots) & (size > 0) & (end + size <= WINDOW)
                starts.append(jnp.where(going, end, WINDOW))
                lasts.append(jnp.where(going, end + meta[slot + k], WINDOW))
                end = jnp.where(going, end + size, end)
                ends.append(jnp.where(going, end, WINDOW))
                count = jnp.where(going, count + 1, count)
            small(first, starts, ends, lasts)
            return slot + count, first + end

        return lax.cond(rows == B3, take_big, take_small)

    lax.while_loop(more, step, (jnp.int32(0), jnp.int32(0)))


def slot_ids(ids, starts, stops, outside):
    result = jnp.full(ids.shape, outside, jnp.int32)
    for k in range(4):
        result = jnp.where((ids >= starts[k]) & (ids < stops[k]), k, result)
    return result


def attention_kernel(
    slots,
    meta,
    own_ref,
    tokens_ref,
    mark_ref,
    vec_ref,
    w_ref,
    heads_own_ref,
    heads_other_ref,
    qkv_ref,
    normed_ref,
    x_ref,
    mixed_ref,
):
    pairs = own_ref.shape[1]
    half = own_ref.shape[2]
    total = 2 * half
    first_own = pl.multiple_of(meta[64], half)
    first_other = pl.multiple_of(half - meta[64], half)

    def store(c, p, first, value):
        begin = pl.multiple_of(first_other + first, WINDOW)
        qkv_ref[c, p, pl.ds(begin, value.shape[0]), :] = value

    project_rows(tokens_ref, mark_ref, vec_ref, w_ref, normed_ref, x_ref, store)
    for c in range(3):
        for p in range(pairs):
            qkv_ref[c, p, pl.ds(first_own, half), :] = own_ref[c, p]
            qkv_ref[c, p, pl.ds(total, WINDOW), :] = jnp.zeros((WINDOW, 128), BF16)
    mixed_ref[...] = jnp.zeros(mixed_ref.shape, BF16)
    low = lax.broadcasted_iota(jnp.int32, (1, 128), 1) < HEAD_DIM
    lanes = (low, jnp.logical_not(low))

    def mix(chosen, first, count, window, mask):
        scores = []
        for p in chosen:
            q = qkv_ref[0, p, pl.ds(first, count), :]
            keys = qkv_ref[1, p, window, :]
            for h in range(2):
                scores.append(nt(jnp.where(lanes[h], q, 0), keys))
        probs = []
        for score in scores:
            score = jnp.where(mask, score, masked_score)
            exponent = jnp.exp(score - jnp.max(score, axis=1, keepdims=True))
            inverse = 1.0 / jnp.sum(exponent, axis=1, keepdims=True)
            probs.append((exponent * inverse).astype(BF16))
        for k, p in enumerate(chosen):
            values = qkv_ref[2, p, window, :]
            mixed = jnp.where(low, nn(probs[2 * k], values), nn(probs[2 * k + 1], values))
            mixed_ref[p, pl.ds(first, count), :] = mixed.astype(BF16)

    def small(first, starts, ends, lasts):
        row = slot_ids(lax.broadcasted_iota(jnp.int32, (WINDOW, 1), 0), starts, ends, 4)
        column = slot_ids(lax.broadcasted_iota(jnp.int32, (1, WINDOW), 1), starts, lasts, 5)
        mix(range(pairs), first, WINDOW, pl.ds(first, WINDOW), row == column)

    def big(first, length):
        mask = lax.broadcasted_iota(jnp.int32, (1, B3), 1) < length

        def block(b, carry):
            begin = pl.multiple_of(first + b * BIG_ROWS, 16)
            mix(range(pairs), begin, BIG_ROWS, pl.ds(first, B3), mask)
            return carry

        lax.fori_loop(0, pl.cdiv(B3, BIG_ROWS), block, 0)

    walk_groups(meta, slots, small, big)
    for p in range(pairs):
        heads_own_ref[:, p * 128 : (p + 1) * 128] = mixed_ref[p, pl.ds(first_own, half), :]
        heads_other_ref[:, p * 128 : (p + 1) * 128] = mixed_ref[p, pl.ds(first_other, half), :]


def attention_back_kernel(
    slots, meta, qkv_ref, own_ref, other_ref, w_ref, grad_ref, out_ref, sum_ref
):
    pairs = qkv_ref.shape[1]
    half = own_ref.shape[0]
    total = 2 * half
    first_own = pl.multiple_of(meta[64], half)
    first_other = pl.multiple_of(half - meta[64], half)
    for source, first in ((own_ref, first_own), (other_ref, first_other)):
        part = nt(source[...], w_ref[...]).astype(BF16)
        for p in range(pairs):
            out_ref[p, pl.ds(first, half), :] = part[:, p * 128 : (p + 1) * 128]
    for p in range(pairs):
        out_ref[p, pl.ds(total, WINDOW), :] = jnp.zeros((WINDOW, 128), BF16)
    grad_ref[...] = jnp.zeros(grad_ref.shape, BF16)
    low = lax.broadcasted_iota(jnp.int32, (1, 128), 1) < HEAD_DIM
    lanes = (low, jnp.logical_not(low))

    def back(chosen, first, count, window, mask, rows_in):
        work = []
        for p in chosen:
            q = qkv_ref[0, p, pl.ds(first, count), :]
            keys = qkv_ref[1, p, window, :]
            values = qkv_ref[2, p, window, :]
            grads = out_ref[p, pl.ds(first, count), :]
            if rows_in is not None:
                grads = jnp.where(rows_in, grads, 0)
            for h in range(2):
                q_h = jnp.where(lanes[h], q, 0)
                g_h = jnp.where(lanes[h], grads, 0)
                work.append((nt(keys, q_h), nt(values, g_h), q_h, g_h))
        pieces = []
        for scores, grad_probs, q_h, g_h in work:
            scores = jnp.where(mask, scores, masked_score)
            exponent = jnp.exp(scores - jnp.max(scores, axis=0, keepdims=True))
            probs = exponent * (1.0 / jnp.sum(exponent, axis=0, keepdims=True))
            inner = jnp.sum(probs * grad_probs, axis=0, keepdims=True)
            grad_scores = (probs * (grad_probs - inner)).astype(BF16)
            pieces.append((probs.astype(BF16), grad_scores, q_h, g_h))
        results = []
        for k, p in enumerate(chosen):
            keys = qkv_ref[1, p, window, :]
            d_query = d_key = d_value = 0.0
            for h in range(2):
                probs, grad_scores, q_h, g_h = pieces[2 * k + h]
                d_query = d_query + tn(grad_scores, jnp.where(lanes[h], keys, 0))
                d_key = d_key + nn(grad_scores, q_h)
                d_value = d_value + nn(probs, g_h)
            grad_ref[0, p, pl.ds(first, count), :] = (d_query * 0.125).astype(BF16)
            results.append((d_key, d_value))
        return results

    def small(first, starts, ends, lasts):
        key = slot_ids(lax.broadcasted_iota(jnp.int32, (WINDOW, 1), 0), starts, lasts, 5)
        query = slot_ids(lax.broadcasted_iota(jnp.int32, (1, WINDOW), 1), starts, ends, 4)
        rows_in = slot_ids(lax.broadcasted_iota(jnp.int32, (WINDOW, 1), 0), starts, ends, 4) < 4
        window = pl.ds(first, WINDOW)
        parts = back(range(pairs), first, WINDOW, window, key == query, rows_in)
        for p, (d_key, d_value) in enumerate(parts):
            grad_ref[1, p, window, :] = d_key.astype(BF16)
            grad_ref[2, p, window, :] = d_value.astype(BF16)

    def big(first, length):
        mask = lax.broadcasted_iota(jnp.int32, (B3, 1), 0) < length
        window = pl.ds(first, B3)
        sum_ref[...] = jnp.zeros(sum_ref.shape, F32)

        def block(b, carry):
            begin = pl.multiple_of(first + b * BIG_ROWS, 16)
            rows_in = lax.broadcasted_iota(jnp.int32, (BIG_ROWS, 1), 0) < B3 - b * BIG_ROWS
            for p, parts in enumerate(back(range(pairs), begin, BIG_ROWS, window, mask, rows_in)):
                for c in range(2):
                    sum_ref[c, p] += parts[c]
            return carry

        lax.fori_loop(0, pl.cdiv(B3, BIG_ROWS), block, 0)
        for p in range(pairs):
            for c in range(2):
                grad_ref[1 + c, p, window, :] = sum_ref[c, p].astype(BF16)

    walk_groups(meta, slots, small, big)


def feed_kernel(
    keep_attn,
    meta,
    mine_ref,
    theirs_ref,
    x_ref,
    gb_ref,
    vec_ref,
    wp_ref,
    wp_first_ref,
    wp_second_ref,
    w1_ref,
    w2_ref,
    normed_ref,
    act_ref,
    gpre_ref,
    grad_ref,
    *more,
):
    units = w1_ref.shape[1]
    step = x_ref.shape[1]
    sum_ref = more[-1]
    even = meta[65] == 0
    wp_theirs = jnp.concatenate(
        [
            jnp.where(even, wp_first_ref[...], wp_second_ref[...]),
            jnp.where(even, wp_second_ref[...], wp_first_ref[...]),
        ],
        axis=1,
    )

    def block(rows, carry):
        attn = nn(mine_ref[rows, :], wp_ref[...]) + nn(theirs_ref[rows, :], wp_theirs)
        attn = attn + row_of(vec_ref, 6)
        if keep_attn:
            more[0][rows, :] = attn
        hidden = x_ref[rows, :].astype(F32) + row_of(vec_ref, 4) * attn
        normal, inverse = normed_of(hidden)
        normed = (normal * row_of(vec_ref, 2) + row_of(vec_ref, 3)).astype(BF16)
        normed_ref[rows, :] = normed
        sum_ref[...] = jnp.zeros(sum_ref.shape, F32)

        def chunk(u, carry):
            cols = pl.ds(pl.multiple_of(u * step, step), step)
            shift = row_of(vec_ref, 10)
            for k in range(1, units // step):
                shift = jnp.where(u == k, row_of(vec_ref, 10 + k), shift)
            pre = nn(normed_ref[rows, :], w1_ref[:, cols]) + shift
            half_phi = 0.5 * (1.0 + lax.erf(pre * 0.7071067811865476))
            act_ref[rows, cols] = (pre * half_phi).astype(BF16)
            slope = half_phi + pre * (jnp.exp(pre * pre * -0.5) * 0.3989422804014327)
            gpre = (nt(gb_ref[rows, :], w2_ref[cols, :]) * slope).astype(BF16)
            gpre_ref[rows, cols] = gpre
            sum_ref[...] += nt(gpre, w1_ref[:, cols])
            return carry

        lax.fori_loop(0, units // step, chunk, 0)
        grad_ref[rows, :] = sum_ref[...].astype(BF16)

    block(pl.ds(0, x_ref.shape[0]), 0)


def feed_grad_kernel(
    n_own, n_other, a_own, a_other, p_own, p_other, g_own, g_other, fc1_ref, fc2_ref, bias_ref
):
    units = a_own.shape[1]
    tile = 512

    def block(i, carry):
        cols = pl.ds(pl.multiple_of(i * tile, tile), tile)
        fc1_ref[:, cols] = (
            tn(n_own[...], p_own[:, cols]) + tn(n_other[...], p_other[:, cols])
        ).astype(BF16)
        fc2_ref[cols, :] = (
            tn(a_own[:, cols], g_own[...]) + tn(a_other[:, cols], g_other[...])
        ).astype(BF16)
        bias_ref[:, cols] = jnp.sum(p_own[:, cols].astype(F32), axis=0, keepdims=True) + jnp.sum(
            p_other[:, cols].astype(F32), axis=0, keepdims=True
        )
        return carry

    lax.fori_loop(0, units // tile, block, 0)


def feed_grads(n_own, n_other, a_own, a_other, p_own, p_other, g_own, g_other):
    units = a_own.shape[1]
    width = n_own.shape[1]
    return call(
        feed_grad_kernel,
        [shape((width, units)), shape((units, width)), shape((1, units), F32)],
        (n_own, n_other, a_own, a_other, p_own, p_other, g_own, g_other),
        0.3,
        "feed_grads",
    )


def branch_kernel(act_ref, w2_ref, out_ref):
    def block(rows, carry):
        out_ref[rows, :] = nn(act_ref[rows, :], w2_ref[...]).astype(out_ref.dtype)

    over_rows(act_ref.shape[0], block)


def middle_kernel(
    begin, mine_ref, got_ref, attn_ref, x_ref, gout_ref, vec_ref, hidden_ref, ga_ref, sum_ref
):
    rows = pl.ds(begin, got_ref.shape[0])
    attn = attn_ref[rows, :]
    normal, inverse = normed_of(x_ref[rows, :].astype(F32) + row_of(vec_ref, 4) * attn)
    grad = mine_ref[rows, :].astype(F32) + got_ref[...].astype(F32)
    grad_hidden = gout_ref[rows, :].astype(F32) + norm_back(grad, row_of(vec_ref, 2), normal, inverse)
    hidden_ref[...] = grad_hidden
    grad_attn = (row_of(vec_ref, 4) * grad_hidden).astype(BF16)
    ga_ref[...] = grad_attn
    sums = [
        jnp.sum(v, axis=0, keepdims=True)
        for v in (grad * normal, grad, grad_hidden * attn, grad_attn.astype(F32))
    ]
    for k in range(4):
        sum_ref[k : k + 1, :] = sums[k]


def share_kernel(meta, grad_ref, w_ref, own_ref, other_ref):
    pairs = grad_ref.shape[1]
    half = own_ref.shape[0]
    for first, target in ((half - meta[64], other_ref), (meta[64], own_ref)):

        def block(to_rows, carry):
            rows = pl.ds(pl.multiple_of(first + to_rows.start, WINDOW), WINDOW)
            total = None
            for c in range(3):
                wide = jnp.concatenate([grad_ref[c, p, rows, :] for p in range(pairs)], axis=1)
                part = nt(wide, w_ref[c])
                total = part if total is None else total + part
            target[to_rows, :] = total.astype(BF16)

        over_rows(half, block)


def weight_kernel(
    meta, grad_ref, n_own, n_other, h_own, h_other, g_own, g_other, keep_ref, give_ref, bias_ref
):
    pairs = grad_ref.shape[1]
    half = n_own.shape[0]
    local = pairs * 128
    own = pl.ds(pl.multiple_of(meta[64], half), half)
    other = pl.ds(pl.multiple_of(half - meta[64], half), half)
    grads = []
    for c in range(3):
        wide_own = jnp.concatenate([grad_ref[c, p, own, :] for p in range(pairs)], axis=1)
        wide_other = jnp.concatenate([grad_ref[c, p, other, :] for p in range(pairs)], axis=1)
        bias_ref[c : c + 1, :] = jnp.sum(wide_own.astype(F32), axis=0, keepdims=True) + jnp.sum(
            wide_other.astype(F32), axis=0, keepdims=True
        )
        grads.append((wide_own, wide_other))
    for k, out_ref in enumerate((keep_ref, give_ref)):
        half_id = meta[65] if k == 0 else 1 - meta[65]
        columns = pl.ds(pl.multiple_of(half_id * local, local), local)
        for c in range(3):
            part = tn(n_own[:, columns], grads[c][0]) + tn(n_other[:, columns], grads[c][1])
            out_ref[pl.ds(c * local, local), :] = part.astype(BF16)
        part = tn(h_own[...], g_own[:, columns]) + tn(h_other[...], g_other[:, columns])
        out_ref[pl.ds(3 * local, local), :] = part.astype(BF16)


def final_kernel(
    mine_ref, got_ref, x_ref, hidden_ref, mark_ref, vec_ref, tokens_ref, sum_ref
):
    sums = [jnp.zeros((1, x_ref.shape[1]), F32)] * 3
    for first in range(0, x_ref.shape[0], WINDOW):
        rows = pl.ds(first, WINDOW)
        normal, inverse = normed_of(x_ref[rows, :].astype(F32))
        grad = mine_ref[rows, :].astype(F32) + got_ref[rows, :].astype(F32)
        grad_x = hidden_ref[rows, :] + norm_back(grad, row_of(vec_ref, 0), normal, inverse)
        marked = mark_ref[rows, :] > 0.5
        tokens_ref[rows, :] = jnp.where(marked, 0.0, grad_x)
        parts = [
            jnp.sum(v, axis=0, keepdims=True)
            for v in (jnp.where(marked, grad_x, 0.0), grad * normal, grad)
        ]
        sums = [a + b for a, b in zip(sums, parts)]
    for k in range(3):
        sum_ref[k : k + 1, :] = sums[k]


def unpack_kernel(count, meta, mine_ref, core_ref, *refs):
    vector_refs, pair_ref, units_ref = refs[-2 - count : -2], refs[-2], refs[-1]
    qkv_ref, proj_ref = refs[8:10]
    total = mine_ref[...] + core_ref[...]
    for k, ref in enumerate(vector_refs):
        ref[...] = total[k]
    width, local = total.shape[1], qkv_ref.shape[2]
    for k in range(2):
        pair_ref[k : k + 1, :] = total[count : count + 1, k * local : (k + 1) * local]
    for k in range(count + 1, total.shape[0]):
        units_ref[pl.ds((k - count - 1) * width, width)] = total[k]
    for k, ref in enumerate(refs[:8]):
        begin = pl.ds(pl.multiple_of((meta[65] ^ (k % 2)) * local, local), local)
        block = (meta[66] ^ (k // 2 % 2)) * 2 + (meta[67] ^ (k // 4))

        @pl.when(block < 3)
        def first(ref=ref, begin=begin, block=block):
            qkv_ref[block, begin, :] = ref[...].astype(F32)

        @pl.when(block == 3)
        def second(ref=ref, begin=begin):
            proj_ref[:, begin] = ref[...].astype(F32)


def own_validity(lengths, buckets, first_own, own_rows):
    slots = lengths.shape[0]
    rows = jnp.where(buckets == 0, B0, jnp.where(buckets == 1, B1, jnp.where(buckets == 2, B2, B3)))
    padded = jnp.where(lengths > 0, rows, 0).astype(jnp.int32)
    before = jnp.tril(jnp.ones((slots, slots), jnp.int32), -1)
    starts = jnp.sum(before * padded[None, :], axis=1)
    ids = first_own + lax.broadcasted_iota(jnp.int32, (own_rows, slots), 0)
    inside = (ids >= starts[None, :]) & (ids < (starts + lengths)[None, :])
    return jnp.any(inside, axis=1, keepdims=True)


def chip_bits():
    return list(range(1, lax.axis_size("wide").bit_length() - 1))


def hop(value, flip):
    size = lax.axis_size("wide")
    return lax.ppermute(value, "wide", tuple((i, i ^ flip) for i in range(size)))


def bits_at(shift, count=1):
    return ((lax.axis_index("wide") >> shift) % (1 << count)).astype(jnp.int32)


def fold_kernel(parts, place, meta, mine_ref, got_ref, *out_refs):
    rows = out_refs[0].shape[0]
    for flip, out_ref in enumerate(out_refs):
        start = pl.multiple_of((meta[place] ^ flip) * rows, rows)
        total = mine_ref[pl.ds(start, rows), :].astype(F32) + got_ref[pl.ds(start, rows), :].astype(F32)
        out_ref[...] = total.astype(BF16)


def fold(meta, mine, got, parts, place, index):
    rows = mine.shape[0] // parts
    if rows % 32:
        total = (mine.astype(F32) + got.astype(F32)).astype(BF16)
        return [
            lax.dynamic_slice_in_dim(total, (index ^ flip) * rows, rows) for flip in range(parts)
        ]
    return call(
        partial(fold_kernel, parts, place),
        [shape((rows, mine.shape[1]))] * parts,
        (meta, mine, got),
        1,
        "fold",
        scalars=1,
    )


def gather_kernel(place, meta, *refs):
    out_ref = refs[-1]
    rows = refs[0].shape[0]
    for flip, ref in enumerate(refs[:-1]):
        start = pl.multiple_of((meta[place] ^ flip) * rows, rows)
        out_ref[pl.ds(start, rows), :] = ref[...]


def gather(meta, pieces, place, index):
    rows, columns = pieces[0].shape
    if rows % 32:
        total = jnp.zeros((rows * len(pieces), columns), pieces[0].dtype)
        for flip, piece in enumerate(pieces):
            total = lax.dynamic_update_slice_in_dim(total, piece, (index ^ flip) * rows, 0)
        return total
    return call(
        partial(gather_kernel, place),
        shape((rows * len(pieces), columns)),
        (meta, *pieces),
        1,
        "gather",
        scalars=1,
    )


def quarter(w_proj, bit):
    rows, columns = w_proj.shape[0] // 2, w_proj.shape[1] // 2
    part = lax.dynamic_slice(w_proj, (bits_at(bit) * rows, bits_at(0) * columns), (rows, columns))
    return lax.ppermute(part, "narrow", SWAP)


def shards(
    tokens,
    token_marks,
    crop_lengths,
    bucket_ids,
    mask_token,
    norm1_gain,
    norm1_bias,
    w_qkv,
    qv_bias,
    w_proj,
    proj_bias,
    scale_attn,
    norm2_gain,
    norm2_bias,
    w_fc1,
    fc1_bias,
    w_fc2,
    fc2_bias,
    scale_mlp,
    cotangent,
):
    half, width = tokens.shape
    slots = crop_lengths.shape[0]
    local = w_qkv.shape[2]
    pairs = local // 128
    units = w_fc1.shape[1]
    first_own = (lax.axis_index("narrow") * half).astype(jnp.int32)
    swap = lambda v: lax.ppermute(v, "narrow", SWAP)
    singles = chip_bits()

    tokens_other = swap(tokens)
    marks_other = swap(token_marks)
    valid = own_validity(crop_lengths, bucket_ids, first_own, half)
    scale2 = scale_mlp.astype(F32)
    gout_own = jnp.where(valid, cotangent, 0).astype(BF16)
    gb_own = (scale2 * gout_own.astype(F32)).astype(BF16)
    pad = jnp.zeros((32 - slots,), jnp.int32)
    meta = jnp.concatenate(
        [
            crop_lengths,
            pad,
            bucket_ids,
            pad,
            jnp.stack(
                [first_own, bits_at(0)] + [bits_at(bit) for bit in singles]
            ),
        ]
    )
    table = [
        norm1_gain,
        norm1_bias,
        norm2_gain,
        norm2_bias,
        scale_attn,
        scale_mlp,
        proj_bias,
        fc2_bias,
        mask_token,
        qv_bias.reshape(width),
    ] + [fc1_bias[k * width : (k + 1) * width] for k in range(units // width)]
    lines = lax.broadcasted_iota(jnp.int32, (len(table), width), 0)
    vec = jnp.zeros((len(table), width), BF16)
    for k, line in enumerate(table):
        vec = jnp.where(lines == k, line[None, :], vec)

    def qkv(rows, marks):
        return call(
            qkv_kernel,
            [shape((half, width)), shape((3, pairs, half, 128)), shape((half, width))],
            (rows, marks, vec, w_qkv),
            2,
            "norm_qkv",
        )

    mark_column = (token_marks == 1).astype(F32)[:, None]
    n_own, qkv_own, x_own = qkv(tokens, mark_column)
    n_own, wp_start = lax.optimization_barrier((n_own, w_proj))
    wp_mine = quarter(wp_start, singles[0])
    tokens_other, gb_start = lax.optimization_barrier((tokens_other, gb_own))
    gb_other = swap(gb_start)
    heads_own, heads_other, qkv_all, n_other, x_other = call(
        partial(attention_kernel, slots),
        [
            shape((half, local)),
            shape((half, local)),
            shape((3, pairs, 2 * half + WINDOW, 128)),
            shape((half, width)),
            shape((half, width)),
        ],
        (meta, qkv_own, tokens_other, (marks_other == 1).astype(F32)[:, None], vec, w_qkv),
        12,
        "attention",
        scratch=[pltpu.VMEM((pairs, 2 * half + WINDOW, 128), BF16)],
        scalars=1,
    )
    heads_own, heads_other, wp_mine = lax.optimization_barrier((heads_own, heads_other, wp_mine))
    wp_side = hop(wp_mine, 1 << singles[0])
    heads_own, heads_other, gb_other, wp_side = lax.optimization_barrier(
        (heads_own, heads_other, gb_other, wp_side)
    )
    got_other = swap(heads_own)
    got_own = swap(heads_other)
    wp_mine = gather(meta, [wp_mine, wp_side], 66, bits_at(singles[0]))
    wp_next = hop(wp_mine, 1)

    def feed(mine, theirs, x, gb, keep):
        outs = [shape((half, width)), shape((half, units)), shape((half, units)), shape((half, width))]
        if keep:
            outs.append(shape((half, width), F32))
        return call(
            partial(feed_kernel, keep),
            outs,
            (meta, mine, theirs, x, gb, vec, w_proj, wp_mine, wp_next, w_fc1, w_fc2),
            7,
            "feed",
            scratch=[pltpu.VMEM((half, width), F32)],
            scalars=1,
        )

    n2_other, act_other, gpre_other, gn2_other = feed(
        heads_other, got_other, x_other, gb_other, False
    )
    gn2_got = swap(gn2_other)
    n2_own, act_own, gpre_own, gn2_own, attn_own = feed(
        heads_own, got_own, x_own, gb_own, True
    )
    g_fc1, g_fc2, g_fc1b = feed_grads(
        n2_own, n2_other, act_own, act_other, gpre_own, gpre_other, gb_own, gb_other
    )
    gn2_got, g_fc1, g_fc2 = lax.optimization_barrier((gn2_got, g_fc1, g_fc2))
    grad_hidden, ga_own, sums2 = call(
        partial(middle_kernel, 0),
        [shape((half, width), F32), shape((half, width)), shape((4, width), F32)],
        (gn2_own, gn2_got, attn_own, x_own, gout_own, vec),
        0.2,
        "middle",
    )
    sum_fc1, sum_fc2 = lax.psum((g_fc1, g_fc2), "wide")

    operands = (
        attn_own, x_own, gout_own, gb_own, act_own, act_other, qkv_all, n_own, n_other,
        heads_own, heads_other, g_fc1b, grad_hidden, ga_own, sums2
    )

    def rest(operands):
        (
            attn_own, x_own, gout_own, gb_own, act_own, act_other, qkv_all, n_own, n_other, heads_own, heads_other, g_fc1b, grad_hidden, ga_own, sums2
        ) = operands
        ga_other = swap(ga_own)

        def branch_of(act, kind):
            return call(
                branch_kernel, shape((half, width), kind), (act, w_fc2), 2, "branch"
            )

        branch_got = swap(branch_of(act_other, BF16))
        branch_own = branch_of(act_own, F32)
        ga_other, branch_own = lax.optimization_barrier((ga_other, branch_own))
        ga = (ga_own, ga_other)
        d_qkv = call(
            partial(attention_back_kernel, slots),
            shape((3, pairs, 2 * half + WINDOW, 128)),
            (meta, qkv_all, *ga, w_proj),
            9,
            "attention_back",
            scratch=[
                pltpu.VMEM((pairs, 2 * half + WINDOW, 128), BF16),
                pltpu.VMEM((2, pairs, B3, 128), F32),
            ],
            scalars=1,
        )
        d_qkv, branch_got = lax.optimization_barrier((d_qkv, branch_got))
        keep, give, d_bias = call(
            weight_kernel,
            [shape((2 * width, local)), shape((2 * width, local)), shape((3, local), F32)],
            (meta, d_qkv, n_own, n_other, heads_own, heads_other, *ga),
            4,
            "weights",
            scalars=1,
        )
        d_qkv, keep, give = lax.optimization_barrier((d_qkv, keep, give))
        got = hop(give, 1)
        gn1_own, gn1_other = call(
            share_kernel,
            [shape((half, width)), shape((half, width))],
            (meta, d_qkv, w_qkv),
            3,
            "share",
            scalars=1,
        )
        gn1_got = swap(gn1_other)
        got, gn1_own = lax.optimization_barrier((got, gn1_own))
        branch = branch_own + branch_got.astype(F32) + fc2_bias.astype(F32)
        hidden = x_own.astype(F32) + scale_attn.astype(F32) * attn_own
        output = jnp.where(valid, hidden + scale2 * branch, 0.0).astype(BF16)
        g_smlp = jnp.sum(gout_own.astype(F32) * branch, axis=0)
        g_fc2b = jnp.sum(gb_own.astype(F32), axis=0)
        for k, bit in enumerate(singles):
            keep, give = fold(meta, keep, got, 2, 66 + k, bits_at(bit))
            got = hop(give, 1 << bit)
            if k == 0:
                got, output, g_smlp, g_fc2b = lax.optimization_barrier((got, output, g_smlp, g_fc2b))
        keep, gn1_got = lax.optimization_barrier((keep, gn1_got))
        grad_tokens, sums1 = call(
            final_kernel,
            [shape((half, width), F32), shape((3, width), F32)],
            (gn1_own, gn1_got, x_own, grad_hidden, mark_column, vec),
            3,
            "final",
        )
        got, grad_tokens = lax.optimization_barrier((got, grad_tokens))
        part = (keep.astype(F32) + got.astype(F32)).astype(BF16)
        wide_only = jnp.concatenate([d_bias[0], d_bias[2], g_fc1b[0]]).reshape(-1, width)
        small = jnp.concatenate([sums1, sums2, g_fc2b[None], g_smlp[None], wide_only], axis=0)
        for k in range(len(singles) - 1, 1, -1):
            part, small = lax.optimization_barrier((part, small))
            pieces = [part, hop(part, 1 << singles[k])]
            small = small + hop(small, 1 << singles[k])
            part = gather(meta, pieces, 66 + k, bits_at(singles[k]))
        part, small = lax.optimization_barrier((part, small))
        side, near = 1 << singles[0], 1 << singles[1]
        next_part, beside, across = hop(part, near), hop(part, side), hop(part, 1)
        small = small + hop(small, near)
        next_part, beside, across, small = lax.optimization_barrier((next_part, beside, across, small))
        next_beside, next_across, corner = hop(next_part, side), hop(next_part, 1), hop(beside, 1)
        count = 9
        flip = 2 * side + 1
        size = 2 * lax.axis_size("wide")
        opposite = lax.ppermute(
            small[:count], ("wide", "narrow"), tuple((i, i ^ flip) for i in range(size))
        )
        shared = small[:count] + swap(small[:count]) + opposite
        small = jnp.concatenate([shared, small[count:]], axis=0) + hop(small, side)
        next_beside, next_across, corner, small = lax.optimization_barrier(
            (next_beside, next_across, corner, small)
        )
        next_corner = hop(next_beside, 1)
        g_qkv, g_proj, *vectors, g_qvb, g_fc1b = call(
            partial(unpack_kernel, count),
            [shape((3, width, local), F32), shape((local, width), F32)]
            + [shape((width,), F32)] * count
            + [shape((2, local), F32), shape((units,), F32)],
            (meta, small, hop(small, 1), part, across, beside, corner, next_part, next_across, next_beside, next_corner),
            3,
            "unpack",
            scalars=1,
        )
        return output, grad_tokens, vectors, g_qvb, g_fc1b, g_qkv, g_proj

    def none(operands):
        return jax.tree.map(lambda v: jnp.zeros(v.shape, v.dtype), jax.eval_shape(rest, operands))

    output, grad_tokens, rows, g_qvb, g_fc1b, g_qkv, g_proj = lax.cond(
        jnp.max(crop_lengths) < 65536, rest, none, operands
    )
    return (
        output,
        grad_tokens,
        rows[0],
        rows[1],
        rows[2],
        g_qkv,
        g_qvb,
        g_proj,
        rows[6],
        rows[5],
        rows[3],
        rows[4],
        sum_fc1.astype(F32),
        g_fc1b,
        sum_fc2.astype(F32),
        rows[7],
        rows[8],
    )


def solution(mesh):
    rows = P(("wide", "narrow"), None)
    return jax.shard_map(
        shards,
        mesh=mesh,
        in_specs=(
            rows,
            P(("wide", "narrow")),
            P("wide"),
            P("wide"),
            P(),
            P(),
            P(),
            P(None, None, "narrow"),
            P(None, "narrow"),
            P("narrow", None),
            P(),
            P(),
            P(),
            P(),
            P(None, "narrow"),
            P("narrow"),
            P("narrow", None),
            P(),
            P(),
            rows,
        ),
        out_specs=(
            rows,
            rows,
            P(),
            P(),
            P(),
            P(None, None, "narrow"),
            P(None, "narrow"),
            P("narrow", None),
            P(),
            P(),
            P(),
            P(),
            P(None, "narrow"),
            P("narrow"),
            P("narrow", None),
            P(),
            P(),
        ),
        check_vma=False,
    )
```

profile of v0, /device:TPU:0, one launch (start us, length us, event | category | flops | bytes accessed | tf_op | source)
XLA Modules:
  0.0 243.1 jit_solution(4861714202348573897)
XLA Ops:
  7.2 3.0 %collective-permute-start.22 = (s32[512]{0:T(512)}, s32[512]{0:T(512)S(1)}, u32[]{:S(2)}, u32[]{:S(2)}) collective-permute-start(s32[512]{0:T(512)} %param.23), channel_id=1, source_target_pairs={{0,1},{1,0},{2,3},{3,2},{4,5},{5,4},{6,7},{7,6},{8,9},{9,8},{10,11... | collective-permute-start | bytes 6152 | tf_op jit(solution)/shard_map/ppermute | solution.py:640
  14.8 3.6 %norm_qkv.1 = (bf16[512,768]{1,0:T(8,128)(2,1)}, bf16[3,3,512,128]{3,2,1,0:T(8,128)(2,1)S(1)}, bf16[512,768]{1,0:T(8,128)(2,1)}) custom-call(bf16[512,768]{1,0:T(8,128)(2,1)S(1)} %copy-done.1, f32[512,1]{1,0:T(8,128)S(1)} %copy.40.mark_ref, bf16[12,768]{1,0:T(8,128)(2,1)S(1)} %select_select_fusion.vec_ref, bf16[3,768,384]{2,1,0:T(8,128)(2,1)} %w_ref.3), custom_call_target="tpu_custom_call" | custom-call | flops 2000000000 | bytes 1000 | tf_op jit(solution)/shard_map/norm_qkv/pallas_call | solution.py:66
  22.3 2.3 multiply_convert_fusion
  24.9 6.1 %collective-permute-done.21.tokens_ref = bf16[512,768]{1,0:T(8,128)(2,1)S(1)} collective-permute-done((bf16[512,768]{1,0:T(8,128)(2,1)}, bf16[512,768]{1,0:T(8,128)(2,1)S(1)}, u32[]{:S(2)}, u32[]{:S(2)}) %collective-permute-start.21) | collective-permute-done | bytes 786464 | tf_op jit(solution)/shard_map/ppermute | solution.py:640
  31.0 6.7 %attention.1 = (bf16[512,384]{1,0:T(8,128)(2,1)S(1)}, bf16[512,384]{1,0:T(8,128)(2,1)S(1)}, bf16[3,3,1280,128]{3,2,1,0:T(8,128)(2,1)}, bf16[512,768]{1,0:T(8,128)(2,1)}, bf16[512,768]{1,0:T(8,128)(2,1)S(1)}) custom-call(s32[69]{0:T(128)S(1)} %concatenate.12.meta, bf16[3,3,512,128]{3,2,1,0:T(8,128)(2,1)S(1)} %get-tuple-element.200.own_ref, ...), custom_call_target="tpu_custom_call" | custom-call | flops 12000000000 | bytes 1000 | tf_op jit(solution)/shard_map/attention/pallas_call | solution.py:66
  37.7 3.8 %collective-permute-start.25 = (bf16[192,384]{1,0:T(8,128)(2,1)S(1)}, bf16[192,384]{1,0:T(8,128)(2,1)S(1)}, u32[]{:S(2)}, u32[]{:S(2)}) collective-permute-start(bf16[192,384]{1,0:T(8,128)(2,1)S(1)} %collective-permute-done.23.refs_0_), channel_id=1, source_target_pairs={{0,4},{2,6},{4,0},{6,2},{8,12},{10,14},{12,8},{14,10},{16,20},{18,... | collective-permute-start | bytes 442376 | tf_op jit(solution)/shard_map/ppermute | solution.py:549
  41.5 3.2 %collective-permute-done.25.refs_1_ = bf16[192,384]{1,0:T(8,128)(2,1)S(1)} collective-permute-done((bf16[192,384]{1,0:T(8,128)(2,1)S(1)}, bf16[192,384]{1,0:T(8,128)(2,1)S(1)}, u32[]{:S(2)}, u32[]{:S(2)}) %collective-permute-start.25) | collective-permute-done | bytes 147488 | tf_op jit(solution)/shard_map/ppermute | solution.py:549
  44.7 4.8 %collective-permute-done.24.gb_ref.g_other = bf16[512,768]{1,0:T(8,128)(2,1)S(1)} collective-permute-done((bf16[512,768]{1,0:T(8,128)(2,1)S(1)}, bf16[512,768]{1,0:T(8,128)(2,1)S(1)}, u32[]{:S(2)}, u32[]{:S(2)}) %collective-permute-start.24) | collective-permute-done | bytes 786464 | tf_op jit(solution)/shard_map/ppermute | solution.py:640
  52.2 9.3 %collective-permute-done.28.theirs_ref = bf16[512,384]{1,0:T(8,128)(2,1)S(1)} collective-permute-done((bf16[512,384]{1,0:T(8,128)(2,1)S(1)}, bf16[512,384]{1,0:T(8,128)(2,1)S(1)}, u32[]{:S(2)}, u32[]{:S(2)}) %collective-permute-start.28) | collective-permute-done | bytes 393248 | tf_op jit(solution)/shard_map/ppermute | solution.py:640
  61.6 6.5 %feed.3 = (bf16[512,768]{1,0:T(8,128)(2,1)S(1)}, bf16[512,1536]{1,0:T(8,128)(2,1)S(1)}, bf16[512,1536]{1,0:T(8,128)(2,1)S(1)}, bf16[512,768]{1,0:T(8,128)(2,1)S(1)}) custom-call(s32[69]{0:T(128)S(1)} %concatenate.12.meta, bf16[512,384]{1,0:T(8,128)(2,1)S(1)} %get-tuple-element.211.mine_ref, bf16[512,384]{1,0:T(8,128)(2,1)S(1)} %collective-permute-done.28.theirs_ref, ...), custom_call_target="tpu_custom_call" | custom-call | flops 7000000000 | bytes 1000 | tf_op jit(solution)/shard_map/feed/pallas_call | solution.py:66
  69.0 7.3 %feed.2 = (bf16[512,768]{1,0:T(8,128)(2,1)S(1)}, bf16[512,1536]{1,0:T(8,128)(2,1)S(1)}, bf16[512,1536]{1,0:T(8,128)(2,1)S(1)}, bf16[512,768]{1,0:T(8,128)(2,1)S(1)}, f32[512,768]{1,0:T(8,128)}) custom-call(s32[69]{0:T(128)S(1)} %concatenate.12.meta, bf16[512,384]{1,0:T(8,128)(2,1)S(1)} %get-tuple-element.210.mine_ref, ...), custom_call_target="tpu_custom_call" | custom-call | flops 7000000000 | bytes 1000 | tf_op jit(solution)/shard_map/feed/pallas_call | solution.py:66
  76.3 7.9 %feed_grads.1 = (bf16[768,1536]{1,0:T(8,128)(2,1)}, bf16[1536,768]{1,0:T(8,128)(2,1)}, f32[1,1536]{1,0:T(1,128)}) custom-call(bf16[512,768]{1,0:T(8,128)(2,1)S(1)} %get-tuple-element.218.n_own, bf16[512,768]{1,0:T(8,128)(2,1)S(1)} %get-tuple-element.219.n_other, bf16[512,1536]{1,0:T(8,128)(2,1)S(1)} %get-tuple-element.220.a_own, ...), custom_call_target="tpu_custom_call" | custom-call | flops 300000000 | bytes 1000 | tf_op jit(solution)/shard_map/feed_grads/pallas_call | solution.py:66
  85.4 4.6 %middle.1 = (f32[512,768]{1,0:T(8,128)}, bf16[512,768]{1,0:T(8,128)(2,1)S(1)}, f32[4,768]{1,0:T(4,128)}) custom-call(bf16[512,768]{1,0:T(8,128)(2,1)S(1)} %get-tuple-element.214.mine_ref, bf16[512,768]{1,0:T(8,128)(2,1)S(1)} %collective-permute-done.29.got_ref, f32[512,768]{1,0:T(8,128)} %get-tuple-element.227.attn_ref, ...), custom_call_target="tpu_custom_call" | custom-call | flops 200000000 | bytes 1000 | tf_op jit(solution)/shard_map/middle/pallas_call | solution.py:66
  90.0 138.8 %conditional.1 = (bf16[512,768]{1,0:T(8,128)(2,1)S(1)}, f32[512,768]{1,0:T(8,128)}, f32[768]{0:T(1024)}, f32[768]{0:T(1024)}, f32[768]{0:T(1024)}, /*index=5*/f3...) conditional(s32[]{:T(128)} %convert_element_type.52, () %tuple.32, ...), branch_computations={%region_3.4_spmd, %region_4.7_spmd} | conditional | flops 30006247424 | bytes 105439264 | solution.py:865
  91.4 3.4 %branch.3 = bf16[512,768]{1,0:T(8,128)(2,1)S(1)} custom-call(bf16[512,1536]{1,0:T(8,128)(2,1)S(1)} %get-tuple-element.58.act_ref, bf16[1536,768]{1,0:T(8,128)(2,1)} %get-tuple-element.55.w2_ref), custom_call_target="tpu_custom_call" | custom-call | flops 2000000000 | bytes 1000 | tf_op jit(solution)/shard_map/cond/branch_1_fun/branch/pallas_call | solution.py:66
  97.7 13.0 %collective-permute-done.other_ref.g_other = bf16[512,768]{1,0:T(8,128)(2,1)S(1)} collective-permute-done((bf16[512,768]{1,0:T(8,128)(2,1)S(1)}, bf16[512,768]{1,0:T(8,128)(2,1)S(1)}, u32[]{:S(2)}, u32[]{:S(2)}) %collective-permute-start) | collective-permute-done | bytes 786464 | tf_op jit(solution)/shard_map/cond/branch_1_fun/ppermute | solution.py:640
  112.5 9.3 %collective-permute-done.1 = bf16[512,768]{1,0:T(8,128)(2,1)S(1)} collective-permute-done((bf16[512,768]{1,0:T(8,128)(2,1)S(1)}, bf16[512,768]{1,0:T(8,128)(2,1)S(1)}, u32[]{:S(2)}, u32[]{:S(2)}) %collective-permute-start.1) | collective-permute-done | bytes 786464 | tf_op jit(solution)/shard_map/cond/branch_1_fun/ppermute | solution.py:640
  121.9 4.0 %weights.1 = (bf16[1536,384]{1,0:T(8,128)(2,1)S(1)}, bf16[1536,384]{1,0:T(8,128)(2,1)S(1)}, f32[3,384]{1,0:T(4,128)S(1)}) custom-call(s32[69]{0:T(128)S(1)} %get-tuple-element.51.meta, bf16[3,3,1280,128]{3,2,1,0:T(8,128)(2,1)S(1)} %attention_back.1.grad_ref, bf16[512,768]{1,0:T(8,128)(2,1)S(1)} %copy-done.40, bf16[512,768]{1,0:T(8,128)(2,1)S(1)} %copy-done.41, ...), custom_call_target="tpu_custom_call" | custom-call | flops 4000000000 | bytes 1000 | tf_op jit(solution)/shard_map/cond/branch_1_fun/weights/pallas_call | solution.py:66
  126.0 3.7 %share.1 = (bf16[512,768]{1,0:T(8,128)(2,1)S(1)}, bf16[512,768]{1,0:T(8,128)(2,1)S(1)}) custom-call(s32[69]{0:T(128)S(1)} %get-tuple-element.51.meta, bf16[3,3,1280,128]{3,2,1,0:T(8,128)(2,1)S(1)} %attention_back.1.grad_ref, bf16[3,768,384]{2,1,0:T(8,128)(2,1)S(1)} %copy-done.34), custom_call_target="tpu_custom_call" | custom-call | flops 3000000000 | bytes 1000 | tf_op jit(solution)/shard_map/cond/branch_1_fun/share/pallas_call | solution.py:66
  134.7 13.6 %collective-permute-done.3.got_ref = bf16[768,384]{1,0:T(8,128)(2,1)S(1)} collective-permute-done((bf16[768,384]{1,0:T(8,128)(2,1)S(1)}, bf16[768,384]{1,0:T(8,128)(2,1)S(1)}, u32[]{:S(2)}, u32[]{:S(2)}) %collective-permute-start.3) | collective-permute-done | bytes 589856 | tf_op jit(solution)/shard_map/cond/branch_1_fun/ppermute | solution.py:549
  153.4 9.1 %collective-permute-done.4.got_ref = bf16[384,384]{1,0:T(8,128)(2,1)S(1)} collective-permute-done((bf16[384,384]{1,0:T(8,128)(2,1)S(1)}, bf16[384,384]{1,0:T(8,128)(2,1)S(1)}, u32[]{:S(2)}, u32[]{:S(2)}) %collective-permute-start.4) | collective-permute-done | bytes 294944 | tf_op jit(solution)/shard_map/cond/branch_1_fun/ppermute | solution.py:549
  163.4 5.1 %collective-permute-start.5 = (bf16[192,384]{1,0:T(8,128)(2,1)S(1)}, bf16[192,384]{1,0:T(8,128)(2,1)S(1)}, u32[]{:S(2)}, u32[]{:S(2)}) collective-permute-start(bf16[192,384]{1,0:T(8,128)(2,1)S(1)} %get-tuple-element.88), channel_id=1, source_target_pairs={{0,16},{2,18},{4,20},{6,22},{8,24},{10,26},{12,28},{14,30},{16,0},... | collective-permute-start | bytes 442376 | tf_op jit(solution)/shard_map/cond/branch_1_fun/ppermute | solution.py:549
  168.5 2.6 %final.1 = (f32[512,768]{1,0:T(8,128)}, f32[3,768]{1,0:T(4,128)S(1)}) custom-call(bf16[512,768]{1,0:T(8,128)(2,1)S(1)} %copy-done.3, bf16[512,768]{1,0:T(8,128)(2,1)S(1)} %collective-permute-done.6.got_ref, bf16[512,768]{1,0:T(8,128)(2,1)S(1)} %copy-done.11, f32[512,768]{1,0:T(8,128)S(1)} %copy-done.35, f32[512,1]{1,0:T(8,128)S(1)} %copy.42.mark_ref, ...), custom_call_target="tpu_custom_call" | custom-call | flops 3000000000 | bytes 1000 | tf_op jit(solution)/shard_map/cond/branch_1_fun/final/pallas_call | solution.py:66
  171.2 4.4 %collective-permute-done.5 = bf16[192,384]{1,0:T(8,128)(2,1)S(1)} collective-permute-done((bf16[192,384]{1,0:T(8,128)(2,1)S(1)}, bf16[192,384]{1,0:T(8,128)(2,1)S(1)}, u32[]{:S(2)}, u32[]{:S(2)}) %collective-permute-start.5) | collective-permute-done | bytes 147488 | tf_op jit(solution)/shard_map/cond/branch_1_fun/ppermute | solution.py:549
  175.7 2.9 %collective-permute-start.8 = (f32[12,768]{1,0:T(8,128)S(1)}, f32[12,768]{1,0:T(8,128)S(1)}, u32[]{:S(2)}, u32[]{:S(2)}) collective-permute-start(f32[12,768]{1,0:T(8,128)S(1)} %concatenate.9), channel_id=1, source_target_pairs={{0,16},{2,18},{4,20},{6,22},{8,24},{10,26},{12,28},{14,30},{16,0},... | collective-permute-start | bytes 110600 | tf_op jit(solution)/shard_map/cond/branch_1_fun/ppermute | solution.py:549
  178.6 11.6 %collective-permute-done.8 = f32[12,768]{1,0:T(8,128)S(1)} collective-permute-done((f32[12,768]{1,0:T(8,128)S(1)}, f32[12,768]{1,0:T(8,128)S(1)}, u32[]{:S(2)}, u32[]{:S(2)}) %collective-permute-start.8) | collective-permute-done | bytes 36896 | tf_op jit(solution)/shard_map/cond/branch_1_fun/ppermute | solution.py:549
  190.8 2.4 collective-permute-start.10
  195.3 15.8 %collective-permute-done.12 = f32[12,768]{1,0:T(8,128)S(1)} collective-permute-done((f32[12,768]{1,0:T(8,128)S(1)}, f32[12,768]{1,0:T(8,128)S(1)}, u32[]{:S(2)}, u32[]{:S(2)}) %collective-permute-start.12) | collective-permute-done | bytes 36896 | tf_op jit(solution)/shard_map/cond/branch_1_fun/ppermute | solution.py:549
  217.8 6.2 %collective-permute-done.13.refs_6_ = bf16[384,384]{1,0:T(8,128)(2,1)S(1)} collective-permute-done((bf16[384,384]{1,0:T(8,128)(2,1)S(1)}, bf16[384,384]{1,0:T(8,128)(2,1)S(1)}, u32[]{:S(2)}, u32[]{:S(2)}) %collective-permute-start.13) | collective-permute-done | bytes 294944 | tf_op jit(solution)/shard_map/cond/branch_1_fun/ppermute | solution.py:549
  225.7 3.2 %unpack.1 = (f32[3,768,384]{2,1,0:T(8,128)}, f32[384,768]{1,0:T(8,128)}, f32[768]{0:T(1024)}, f32[768]{0:T(1024)}, f32[768]{0:T(1024)}, /*index=5*/f32[768]{0:T(...) custom-call(s32[69]{0:T(128)S(1)} %copy-done.31, ...), custom_call_target="tpu_custom_call" | custom-call | flops 3000000000 | bytes 1000 | tf_op jit(solution)/shard_map/cond/branch_1_fun/unpack/pallas_call | solution.py:66
  228.9 4.8 %convert_element_type.56 = f32[768,1536]{1,0:T(8,128)} convert(bf16[768,1536]{1,0:T(8,128)(2,1)} %get-tuple-element.304) | non-fusion elementwise | flops 1179648 | bytes 7077888 | tf_op jit(solution)/shard_map/convert_element_type | solution.py:881
  233.7 2.5 %convert_element_type.57 = f32[1536,768]{1,0:T(8,128)} convert(bf16[1536,768]{1,0:T(8,128)(2,1)S(1)} %copy-done.12) | non-fusion elementwise | flops 1179648 | bytes 7077888 | tf_op jit(solution)/shard_map/convert_element_type | solution.py:883
  (179 shorter events, 41.1 us)
Async XLA Ops:
  7.2 221.7 %all-reduce.3.cloned.1.call-start = ((), (), s32[]{:S(2)}) async-start(), calls=%async_computation | async-start | bytes 9437184 | tf_op jit(solution)/shard_map/psum | solution.py:750
  7.2 17.5 %collective-permute-start.22 = (s32[512]{0:T(512)}, s32[512]{0:T(512)S(1)}, u32[]{:S(2)}, u32[]{:S(2)}) collective-permute-start(s32[512]{0:T(512)} %param.23), channel_id=1, source_target_pairs={{0,1},{1,0},{2,3},{3,2},{4,5},{5,4},{6,7},{7,6},{8,9},{9,8},{10,11... | collective-permute-start | bytes 6152 | tf_op jit(solution)/shard_map/ppermute | solution.py:640
  10.3 20.7 %collective-permute-start.21 = (bf16[512,768]{1,0:T(8,128)(2,1)}, bf16[512,768]{1,0:T(8,128)(2,1)S(1)}, u32[]{:S(2)}, u32[]{:S(2)}) collective-permute-start(bf16[512,768]{1,0:T(8,128)(2,1)} %tokens_ref.1), channel_id=1, source_target_pairs={{0,1},{1,0},{2,3},{3,2},{4,5},{5,4},{6,7},{7,6},{8,9},{9,8},{10,11... | collective-permute-start | bytes 2359304 | tf_op jit(solution)/shard_map/ppermute | solution.py:640
  19.4 18.3 %collective-permute-start.23 = (bf16[192,384]{1,0:T(8,128)(2,1)S(1)}, bf16[192,384]{1,0:T(8,128)(2,1)S(1)}, u32[]{:S(2)}, u32[]{:S(2)}) collective-permute-start(bf16[192,384]{1,0:T(8,128)(2,1)S(1)} %dynamic_slice.3), channel_id=1, source_target_pairs={{0,1},{1,0},{2,3},{3,2},{4,5},{5,4},{6,7},{7,6},{8,9},{9,8},{10,11... | collective-permute-start | bytes 442376 | tf_op jit(solution)/shard_map/ppermute | solution.py:609
  30.9 18.5 %collective-permute-start.24 = (bf16[512,768]{1,0:T(8,128)(2,1)S(1)}, bf16[512,768]{1,0:T(8,128)(2,1)S(1)}, u32[]{:S(2)}, u32[]{:S(2)}) collective-permute-start(bf16[512,768]{1,0:T(8,128)(2,1)S(1)} %get-tuple-element.208.gb_ref.g_own), channel_id=1, source_target_pairs={{0,1},{1,0},{2,3},{3,2},{4,5},{5,4},{6,7},{7,6},{8,9},{9,8},{10,11... | collective-permute-start | bytes 2359304 | tf_op jit(solution)/shard_map/ppermute | solution.py:640
  37.7 7.0 %collective-permute-start.25 = (bf16[192,384]{1,0:T(8,128)(2,1)S(1)}, bf16[192,384]{1,0:T(8,128)(2,1)S(1)}, u32[]{:S(2)}, u32[]{:S(2)}) collective-permute-start(bf16[192,384]{1,0:T(8,128)(2,1)S(1)} %collective-permute-done.23.refs_0_), channel_id=1, source_target_pairs={{0,4},{2,6},{4,0},{6,2},{8,12},{10,14},{12,8},{14,10},{16,20},{18,... | collective-permute-start | bytes 442376 | tf_op jit(solution)/shard_map/ppermute | solution.py:549
  49.5 12.1 %collective-permute-start.28 = (bf16[512,384]{1,0:T(8,128)(2,1)S(1)}, bf16[512,384]{1,0:T(8,128)(2,1)S(1)}, u32[]{:S(2)}, u32[]{:S(2)}) collective-permute-start(bf16[512,384]{1,0:T(8,128)(2,1)S(1)} %get-tuple-element.210.mine_ref), channel_id=1, source_target_pairs={{0,1},{1,0},{2,3},{3,2},{4,5},{5,4},{6,7},{7,6},{8,9},{9,8},{10,11... | collective-permute-start | bytes 1179656 | tf_op jit(solution)/shard_map/ppermute | solution.py:640
  50.5 1.8 collective-permute-start.27
  50.5 18.5 %collective-permute-start.26 = (bf16[512,384]{1,0:T(8,128)(2,1)S(1)}, bf16[512,384]{1,0:T(8,128)(2,1)S(1)}, u32[]{:S(2)}, u32[]{:S(2)}) collective-permute-start(bf16[512,384]{1,0:T(8,128)(2,1)S(1)} %get-tuple-element.211.mine_ref), channel_id=1, source_target_pairs={{0,1},{1,0},{2,3},{3,2},{4,5},{5,4},{6,7},{7,6},{8,9},{9,8},{10,11... | collective-permute-start | bytes 1179656 | tf_op jit(solution)/shard_map/ppermute | solution.py:640
  68.1 16.1 %collective-permute-start.29 = (bf16[512,768]{1,0:T(8,128)(2,1)S(1)}, bf16[512,768]{1,0:T(8,128)(2,1)S(1)}, u32[]{:S(2)}, u32[]{:S(2)}) collective-permute-start(bf16[512,768]{1,0:T(8,128)(2,1)S(1)} %get-tuple-element.217), channel_id=1, source_target_pairs={{0,1},{1,0},{2,3},{3,2},{4,5},{5,4},{6,7},{7,6},{8,9},{9,8},{10,11... | collective-permute-start | bytes 2359304 | tf_op jit(solution)/shard_map/ppermute | solution.py:640
  90.1 43.4 %copy-start.10 = (bf16[512,768]{1,0:T(8,128)(2,1)}, bf16[512,768]{1,0:T(8,128)(2,1)S(1)}, u32[]{:S(2)}) copy-start(bf16[512,768]{1,0:T(8,128)(2,1)S(1)} %get-tuple-element.74.x_ref) | copy-start | bytes 2359300 | tf_op jit(solution)/shard_map/cond
  90.1 20.5 %collective-permute-start = (bf16[512,768]{1,0:T(8,128)(2,1)S(1)}, bf16[512,768]{1,0:T(8,128)(2,1)S(1)}, u32[]{:S(2)}, u32[]{:S(2)}) collective-permute-start(bf16[512,768]{1,0:T(8,128)(2,1)S(1)} %get-tuple-element.53.own_ref.g_own), channel_id=1, source_target_pairs={{0,1},{1,0},{2,3},{3,2},{4,5},{5,4},{6,7},{7,6},{8,9},{9,8},{10,11... | collective-permute-start | bytes 2359304 | tf_op jit(solution)/shard_map/cond/branch_1_fun/ppermute | solution.py:640
  94.8 27.0 %collective-permute-start.1 = (bf16[512,768]{1,0:T(8,128)(2,1)S(1)}, bf16[512,768]{1,0:T(8,128)(2,1)S(1)}, u32[]{:S(2)}, u32[]{:S(2)}) collective-permute-start(bf16[512,768]{1,0:T(8,128)(2,1)S(1)} %branch.3), channel_id=1, source_target_pairs={{0,1},{1,0},{2,3},{3,2},{4,5},{5,4},{6,7},{7,6},{8,9},{9,8},{10,11... | collective-permute-start | bytes 2359304 | tf_op jit(solution)/shard_map/cond/branch_1_fun/ppermute | solution.py:640
  125.9 3.8 %collective-permute-start.2 = (bf16[1536,384]{1,0:T(8,128)(2,1)S(1)}, bf16[1536,384]{1,0:T(8,128)(2,1)S(1)}, u32[]{:S(2)}, u32[]{:S(2)}) collective-permute-start(bf16[1536,384]{1,0:T(8,128)(2,1)S(1)} %get-tuple-element.67), channel_id=1, source_target_pairs={{0,2},{2,0},{4,6},{6,4},{8,10},{10,8},{12,14},{14,12},{16,18},{18,... | collective-permute-start | bytes 3538952 | tf_op jit(solution)/shard_map/cond/branch_1_fun/ppermute | solution.py:549
  130.6 17.7 %collective-permute-start.3 = (bf16[768,384]{1,0:T(8,128)(2,1)S(1)}, bf16[768,384]{1,0:T(8,128)(2,1)S(1)}, u32[]{:S(2)}, u32[]{:S(2)}) collective-permute-start(bf16[768,384]{1,0:T(8,128)(2,1)S(1)} %get-tuple-element.72), channel_id=1, source_target_pairs={{0,4},{2,6},{4,0},{6,2},{8,12},{10,14},{12,8},{14,10},{16,20},{18,... | collective-permute-start | bytes 1769480 | tf_op jit(solution)/shard_map/cond/branch_1_fun/ppermute | solution.py:549
  132.9 35.5 %collective-permute-start.6 = (bf16[512,768]{1,0:T(8,128)(2,1)S(1)}, bf16[512,768]{1,0:T(8,128)(2,1)S(1)}, u32[]{:S(2)}, u32[]{:S(2)}) collective-permute-start(bf16[512,768]{1,0:T(8,128)(2,1)S(1)} %get-tuple-element.91), channel_id=1, source_target_pairs={{0,1},{1,0},{2,3},{3,2},{4,5},{5,4},{6,7},{7,6},{8,9},{9,8},{10,11... | collective-permute-start | bytes 2359304 | tf_op jit(solution)/shard_map/cond/branch_1_fun/ppermute | solution.py:640
  149.0 13.5 %collective-permute-start.4 = (bf16[384,384]{1,0:T(8,128)(2,1)S(1)}, bf16[384,384]{1,0:T(8,128)(2,1)S(1)}, u32[]{:S(2)}, u32[]{:S(2)}) collective-permute-start(bf16[384,384]{1,0:T(8,128)(2,1)S(1)} %get-tuple-element.87), channel_id=1, source_target_pairs={{0,8},{2,10},{4,12},{6,14},{8,0},{10,2},{12,4},{14,6},{16,24},{18,... | collective-permute-start | bytes 884744 | tf_op jit(solution)/shard_map/cond/branch_1_fun/ppermute | solution.py:549
  163.4 12.2 %collective-permute-start.5 = (bf16[192,384]{1,0:T(8,128)(2,1)S(1)}, bf16[192,384]{1,0:T(8,128)(2,1)S(1)}, u32[]{:S(2)}, u32[]{:S(2)}) collective-permute-start(bf16[192,384]{1,0:T(8,128)(2,1)S(1)} %get-tuple-element.88), channel_id=1, source_target_pairs={{0,16},{2,18},{4,20},{6,22},{8,24},{10,26},{12,28},{14,30},{16,0},... | collective-permute-start | bytes 442376 | tf_op jit(solution)/shard_map/cond/branch_1_fun/ppermute | solution.py:549
  175.6 14.6 %collective-permute-start.7 = (bf16[192,384]{1,0:T(8,128)(2,1)S(1)}, bf16[192,384]{1,0:T(8,128)(2,1)S(1)}, u32[]{:S(2)}, u32[]{:S(2)}) collective-permute-start(bf16[192,384]{1,0:T(8,128)(2,1)S(1)} %add_convert_fusion.refs_0_), channel_id=1, source_target_pairs={{0,16},{2,18},{4,20},{6,22},{8,24},{10,26},{12,28},{14,30},{16,0},... | collective-permute-start | bytes 442376 | tf_op jit(solution)/shard_map/cond/branch_1_fun/ppermute | solution.py:549
  175.7 14.5 %collective-permute-start.8 = (f32[12,768]{1,0:T(8,128)S(1)}, f32[12,768]{1,0:T(8,128)S(1)}, u32[]{:S(2)}, u32[]{:S(2)}) collective-permute-start(f32[12,768]{1,0:T(8,128)S(1)} %concatenate.9), channel_id=1, source_target_pairs={{0,16},{2,18},{4,20},{6,22},{8,24},{10,26},{12,28},{14,30},{16,0},... | collective-permute-start | bytes 110600 | tf_op jit(solution)/shard_map/cond/branch_1_fun/ppermute | solution.py:549
  190.8 20.3 %collective-permute-start.11 = (bf16[384,384]{1,0:T(8,128)(2,1)S(1)}, bf16[384,384]{1,0:T(8,128)(2,1)S(1)}, u32[]{:S(2)}, u32[]{:S(2)}) collective-permute-start(bf16[384,384]{1,0:T(8,128)(2,1)S(1)} %gather.2.refs_0_), channel_id=1, source_target_pairs={{0,2},{2,0},{4,6},{6,4},{8,10},{10,8},{12,14},{14,12},{16,18},{18,... | collective-permute-start | bytes 884744 | tf_op jit(solution)/shard_map/cond/branch_1_fun/ppermute | solution.py:549
  190.8 20.2 %collective-permute-start.10 = (bf16[384,384]{1,0:T(8,128)(2,1)S(1)}, bf16[384,384]{1,0:T(8,128)(2,1)S(1)}, u32[]{:S(2)}, u32[]{:S(2)}) collective-permute-start(bf16[384,384]{1,0:T(8,128)(2,1)S(1)} %gather.2.refs_0_), channel_id=1, source_target_pairs={{0,4},{2,6},{4,0},{6,2},{8,12},{10,14},{12,8},{14,10},{16,20},{18,... | collective-permute-start | bytes 884744 | tf_op jit(solution)/shard_map/cond/branch_1_fun/ppermute | solution.py:549
  193.2 17.8 %collective-permute-start.9 = (bf16[384,384]{1,0:T(8,128)(2,1)S(1)}, bf16[384,384]{1,0:T(8,128)(2,1)S(1)}, u32[]{:S(2)}, u32[]{:S(2)}) collective-permute-start(bf16[384,384]{1,0:T(8,128)(2,1)S(1)} %gather.2.refs_0_), channel_id=1, source_target_pairs={{0,8},{2,10},{4,12},{6,14},{8,0},{10,2},{12,4},{14,6},{16,24},{18,... | collective-permute-start | bytes 884744 | tf_op jit(solution)/shard_map/cond/branch_1_fun/ppermute | solution.py:549
  194.2 16.9 %collective-permute-start.12 = (f32[12,768]{1,0:T(8,128)S(1)}, f32[12,768]{1,0:T(8,128)S(1)}, u32[]{:S(2)}, u32[]{:S(2)}) collective-permute-start(f32[12,768]{1,0:T(8,128)S(1)} %add.63), channel_id=1, source_target_pairs={{0,8},{2,10},{4,12},{6,14},{8,0},{10,2},{12,4},{14,6},{16,24},{18,... | collective-permute-start | bytes 110600 | tf_op jit(solution)/shard_map/cond/branch_1_fun/ppermute | solution.py:549
  211.1 5.2 %collective-permute-start.17 = (f32[9,768]{1,0:T(8,128)S(1)}, f32[9,768]{1,0:T(8,128)S(1)}, u32[]{:S(2)}, u32[]{:S(2)}) collective-permute-start(f32[9,768]{1,0:T(8,128)S(1)} %bitcast.8), channel_id=1, source_target_pairs={{0,5},{1,4},{2,7},{3,6},{4,1},{5,0},{6,3},{7,2},{8,13},{9,12},{10,... | collective-permute-start | bytes 82952 | tf_op jit(solution)/shard_map/cond/branch_1_fun/ppermute | solution.py:841
  211.6 4.6 %collective-permute-start.16 = (f32[9,768]{1,0:T(8,128)S(1)}, f32[9,768]{1,0:T(8,128)S(1)}, u32[]{:S(2)}, u32[]{:S(2)}) collective-permute-start(f32[9,768]{1,0:T(8,128)S(1)} %bitcast.9), channel_id=1, source_target_pairs={{0,1},{1,0},{2,3},{3,2},{4,5},{5,4},{6,7},{7,6},{8,9},{9,8},{10,11... | collective-permute-start | bytes 82952 | tf_op jit(solution)/shard_map/cond/branch_1_fun/ppermute | solution.py:640
  212.6 4.2 %collective-permute-start.18 = (f32[12,768]{1,0:T(8,128)S(1)}, f32[12,768]{1,0:T(8,128)S(1)}, u32[]{:S(2)}, u32[]{:S(2)}) collective-permute-start(f32[12,768]{1,0:T(8,128)S(1)} %add.64), channel_id=1, source_target_pairs={{0,4},{2,6},{4,0},{6,2},{8,12},{10,14},{12,8},{14,10},{16,20},{18,... | collective-permute-start | bytes 110600 | tf_op jit(solution)/shard_map/cond/branch_1_fun/ppermute | solution.py:549
  214.6 3.2 %collective-permute-start.14 = (bf16[384,384]{1,0:T(8,128)(2,1)S(1)}, bf16[384,384]{1,0:T(8,128)(2,1)S(1)}, u32[]{:S(2)}, u32[]{:S(2)}) collective-permute-start(bf16[384,384]{1,0:T(8,128)(2,1)S(1)} %collective-permute-done.9.refs_4_), channel_id=1, source_target_pairs={{0,2},{2,0},{4,6},{6,4},{8,10},{10,8},{12,14},{14,12},{16,18},{18,... | collective-permute-start | bytes 884744 | tf_op jit(solution)/shard_map/cond/branch_1_fun/ppermute | solution.py:549
  214.6 9.4 %collective-permute-start.13 = (bf16[384,384]{1,0:T(8,128)(2,1)S(1)}, bf16[384,384]{1,0:T(8,128)(2,1)S(1)}, u32[]{:S(2)}, u32[]{:S(2)}) collective-permute-start(bf16[384,384]{1,0:T(8,128)(2,1)S(1)} %collective-permute-done.9.refs_4_), channel_id=1, source_target_pairs={{0,4},{2,6},{4,0},{6,2},{8,12},{10,14},{12,8},{14,10},{16,20},{18,... | collective-permute-start | bytes 884744 | tf_op jit(solution)/shard_map/cond/branch_1_fun/ppermute | solution.py:549
  216.2 1.6 collective-permute-start.15
  224.0 1.7 collective-permute-start.20
  224.0 1.6 collective-permute-start.19
  (42 other events, 405.8 us)
Sparse Core Ops, SparseCore 0:
  84.4 135.5 all-reduce.2
where the time goes:
time: 247 us; the launch traced here: 243 us
  waiting for transfers between devices  111 us (45%)
  Pallas kernels  60.6 us (25%)
  starting transfers between devices  34.7 us (14%)
  other arithmetic  15.6 us (6%)
  between operations  15 us (6%)
  local copies, waits for them, and re-layouts  6.01 us (2%)
    ppermute x18, waiting for transfers between devices, hop(): lax.ppermute(value, 'wide', tuple(((i, i ^ flip) for i in range(size))))  66.5 us
    pallas_call x18, Pallas kernels, call(): pl.pallas_call(kernel, out_shape=out_shape, grid_spec=spec, compiler_para...  60.6 us
    ppermute x10, waiting for transfers between devices, shards(): swap = lambda v: lax.ppermute(v, 'narrow', SWAP)  42.9 us
    ppermute x18, starting transfers between devices, hop(): lax.ppermute(value, 'wide', tuple(((i, i ^ flip) for i in range(size))))  22.3 us
    ppermute x10, starting transfers between devices, shards(): swap = lambda v: lax.ppermute(v, 'narrow', SWAP)  9.79 us
  transfers between devices with their start and end apart: 31, of which 17 were waited for; matrix products, arithmetic and copies ran while one was open for 5% of the time, Pallas kernels for 25%

commit v1 on v0

--- a/solution.py
+++ b/solution.py
@@ -459,30 +459,25 @@
         over_rows(half, block)
 
 
-def weight_kernel(
-    meta, grad_ref, n_own, n_other, h_own, h_other, g_own, g_other, keep_ref, give_ref, bias_ref
-):
+def weight_kernel(flip, meta, grad_ref, n_own, n_other, h_own, h_other, g_own, g_other, *outs):
     pairs = grad_ref.shape[1]
     half = n_own.shape[0]
     local = pairs * 128
     own = pl.ds(pl.multiple_of(meta[64], half), half)
     other = pl.ds(pl.multiple_of(half - meta[64], half), half)
-    grads = []
+    columns = pl.ds(pl.multiple_of((meta[65] ^ flip) * local, local), local)
+    out_ref = outs[0]
     for c in range(3):
         wide_own = jnp.concatenate([grad_ref[c, p, own, :] for p in range(pairs)], axis=1)
         wide_other = jnp.concatenate([grad_ref[c, p, other, :] for p in range(pairs)], axis=1)
-        bias_ref[c : c + 1, :] = jnp.sum(wide_own.astype(F32), axis=0, keepdims=True) + jnp.sum(
-            wide_other.astype(F32), axis=0, keepdims=True
-        )
-        grads.append((wide_own, wide_other))
-    for k, out_ref in enumerate((keep_ref, give_ref)):
-        half_id = meta[65] if k == 0 else 1 - meta[65]
-        columns = pl.ds(pl.multiple_of(half_id * local, local), local)
-        for c in range(3):
-            part = tn(n_own[:, columns], grads[c][0]) + tn(n_other[:, columns], grads[c][1])
-            out_ref[pl.ds(c * local, local), :] = part.astype(BF16)
-        part = tn(h_own[...], g_own[:, columns]) + tn(h_other[...], g_other[:, columns])
-        out_ref[pl.ds(3 * local, local), :] = part.astype(BF16)
+        if flip == 0:
+            outs[1][c : c + 1, :] = jnp.sum(wide_own.astype(F32), axis=0, keepdims=True) + jnp.sum(
+                wide_other.astype(F32), axis=0, keepdims=True
+            )
+        part = tn(n_own[:, columns], wide_own) + tn(n_other[:, columns], wide_other)
+        out_ref[pl.ds(c * local, local), :] = part.astype(BF16)
+    part = tn(h_own[...], g_own[:, columns]) + tn(h_other[...], g_other[:, columns])
+    out_ref[pl.ds(3 * local, local), :] = part.astype(BF16)
 
 
 def final_kernel(
@@ -782,16 +777,26 @@
             scalars=1,
         )
         d_qkv, branch_got = lax.optimization_barrier((d_qkv, branch_got))
-        keep, give, d_bias = call(
-            weight_kernel,
-            [shape((2 * width, local)), shape((2 * width, local)), shape((3, local), F32)],
-            (meta, d_qkv, n_own, n_other, heads_own, heads_other, *ga),
-            4,
-            "weights",
+        arrays = (n_own, n_other, heads_own, heads_other, *ga)
+        (give,) = call(
+            partial(weight_kernel, 1),
+            [shape((2 * width, local))],
+            (meta, d_qkv, *arrays),
+            2,
+            "weights_give",
             scalars=1,
         )
-        d_qkv, keep, give = lax.optimization_barrier((d_qkv, keep, give))
+        d_qkv, give = lax.optimization_barrier((d_qkv, give))
         got = hop(give, 1)
+        keep, d_bias = call(
+            partial(weight_kernel, 0),
+            [shape((2 * width, local)), shape((3, local), F32)],
+            (meta, d_qkv, *arrays),
+            2,
+            "weights_keep",
+            scalars=1,
+        )
+        d_qkv, keep, got = lax.optimization_barrier((d_qkv, keep, got))
         gn1_own, gn1_other = call(
             share_kernel,
             [shape((half, width)), shape((half, width))],
@@ -801,7 +806,6 @@
             scalars=1,
         )
         gn1_got = swap(gn1_other)
-        got, gn1_own = lax.optimization_barrier((got, gn1_own))
         branch = branch_own + branch_got.astype(F32) + fc2_bias.astype(F32)
         hidden = x_own.astype(F32) + scale_attn.astype(F32) * attn_own
         output = jnp.where(valid, hidden + scale2 * branch, 0.0).astype(BF16)
@@ -811,7 +815,9 @@
             keep, give = fold(meta, keep, got, 2, 66 + k, bits_at(bit))
             got = hop(give, 1 << bit)
             if k == 0:
-                got, output, g_smlp, g_fc2b = lax.optimization_barrier((got, output, g_smlp, g_fc2b))
+                got, output, g_smlp, g_fc2b, gn1_own = lax.optimization_barrier(
+                    (got, output, g_smlp, g_fc2b, gn1_own)
+                )
         keep, gn1_got = lax.optimization_barrier((keep, gn1_got))
         grad_tokens, sums1 = call(
             final_kernel,

time: 247 us -> 242 us (0.980); the launches traced: 243 us -> 241 us
  waiting for transfers between devices: 111 us -> 97.5 us
  Pallas kernels: 60.6 us -> 67.2 us
  starting transfers between devices: 34.7 us -> 39.2 us
    ppermute x10, waiting for transfers between devices: 42.9 us -> 35.2 us  [shards(): swap = lambda v: lax.ppermute(v, 'narrow', SWAP)]
    pallas_call x18 -> x19, Pallas kernels: 60.6 us -> 67.2 us  [call(): pl.pallas_call(kernel, out_shape=out_shape, grid_spec=spec, compiler_para...]
    ppermute x18, waiting for transfers between devices: 66.5 us -> 60.5 us  [hop(): lax.ppermute(value, 'wide', tuple(((i, i ^ flip) for i in range(size))))]
    ppermute x18, starting transfers between devices: 22.3 us -> 26.7 us  [hop(): lax.ppermute(value, 'wide', tuple(((i, i ^ flip) for i in range(size))))]
  transfers between devices with their start and end apart: 31 -> 31, of which waited for: 17 -> 17; matrix products, arithmetic and copies ran while one was open for 5% -> 5% of each run, Pallas kernels for 25% -> 28%
where the time goes in v1:
time: 242 us; the launch traced here: 241 us
  waiting for transfers between devices  97.5 us (40%)
  Pallas kernels  67.2 us (28%)
  starting transfers between devices  39.2 us (16%)
  between operations  15.1 us (6%)
  other arithmetic  14.3 us (6%)
  local copies, waits for them, and re-layouts  7.12 us (3%)
    pallas_call x19, Pallas kernels, call(): pl.pallas_call(kernel, out_shape=out_shape, grid_spec=spec, compiler_para...  67.2 us
    ppermute x18, waiting for transfers between devices, hop(): lax.ppermute(value, 'wide', tuple(((i, i ^ flip) for i in range(size))))  60.5 us
    ppermute x10, waiting for transfers between devices, shards(): swap = lambda v: lax.ppermute(v, 'narrow', SWAP)  35.2 us
    ppermute x18, starting transfers between devices, hop(): lax.ppermute(value, 'wide', tuple(((i, i ^ flip) for i in range(size))))  26.7 us
    ppermute x10, starting transfers between devices, shards(): swap = lambda v: lax.ppermute(v, 'narrow', SWAP)  9.7 us
  transfers between devices with their start and end apart: 31, of which 17 were waited for; matrix products, arithmetic and copies ran while one was open for 5% of the time, Pallas kernels for 28%

profile of v1, /device:TPU:0, one launch (start us, length us, event | category | flops | bytes accessed | tf_op | source)
XLA Modules:
  0.0 240.8 jit_solution(2589379761972864830)
XLA Ops:
  7.2 3.0 %collective-permute-start.22 = (s32[512]{0:T(512)}, s32[512]{0:T(512)S(1)}, u32[]{:S(2)}, u32[]{:S(2)}) collective-permute-start(s32[512]{0:T(512)} %param.23), channel_id=1, source_target_pairs={{0,1},{1,0},{2,3},{3,2},{4,5},{5,4},{6,7},{7,6},{8,9},{9,8},{10,11... | collective-permute-start | bytes 6152 | tf_op jit(solution)/shard_map/ppermute | solution.py:635
  14.8 3.6 %norm_qkv.1 = (bf16[512,768]{1,0:T(8,128)(2,1)}, bf16[3,3,512,128]{3,2,1,0:T(8,128)(2,1)S(1)}, bf16[512,768]{1,0:T(8,128)(2,1)}) custom-call(bf16[512,768]{1,0:T(8,128)(2,1)S(1)} %copy-done.1, f32[512,1]{1,0:T(8,128)S(1)} %copy.40.mark_ref, bf16[12,768]{1,0:T(8,128)(2,1)S(1)} %select_select_fusion.vec_ref, bf16[3,768,384]{2,1,0:T(8,128)(2,1)} %w_ref.3), custom_call_target="tpu_custom_call" | custom-call | flops 2000000000 | bytes 1000 | tf_op jit(solution)/shard_map/norm_qkv/pallas_call | solution.py:66
  26.5 4.4 %collective-permute-done.21.tokens_ref = bf16[512,768]{1,0:T(8,128)(2,1)S(1)} collective-permute-done((bf16[512,768]{1,0:T(8,128)(2,1)}, bf16[512,768]{1,0:T(8,128)(2,1)S(1)}, u32[]{:S(2)}, u32[]{:S(2)}) %collective-permute-start.21) | collective-permute-done | bytes 786464 | tf_op jit(solution)/shard_map/ppermute | solution.py:635
  31.0 8.6 %attention.1 = (bf16[512,384]{1,0:T(8,128)(2,1)S(1)}, bf16[512,384]{1,0:T(8,128)(2,1)S(1)}, bf16[3,3,1280,128]{3,2,1,0:T(8,128)(2,1)}, bf16[512,768]{1,0:T(8,128)(2,1)}, bf16[512,768]{1,0:T(8,128)(2,1)S(1)}) custom-call(s32[69]{0:T(128)} %concatenate.12.meta, bf16[3,3,512,128]{3,2,1,0:T(8,128)(2,1)S(1)} %get-tuple-element.200.own_ref, ...), custom_call_target="tpu_custom_call" | custom-call | flops 12000000000 | bytes 1000 | tf_op jit(solution)/shard_map/attention/pallas_call | solution.py:66
  39.6 4.7 %collective-permute-start.25 = (bf16[192,384]{1,0:T(8,128)(2,1)S(1)}, bf16[192,384]{1,0:T(8,128)(2,1)S(1)}, u32[]{:S(2)}, u32[]{:S(2)}) collective-permute-start(bf16[192,384]{1,0:T(8,128)(2,1)S(1)} %collective-permute-done.23.refs_0_), channel_id=1, source_target_pairs={{0,4},{2,6},{4,0},{6,2},{8,12},{10,14},{12,8},{14,10},{16,20},{18,... | collective-permute-start | bytes 442376 | tf_op jit(solution)/shard_map/ppermute | solution.py:544
  44.3 3.1 %collective-permute-done.25.refs_1_ = bf16[192,384]{1,0:T(8,128)(2,1)S(1)} collective-permute-done((bf16[192,384]{1,0:T(8,128)(2,1)S(1)}, bf16[192,384]{1,0:T(8,128)(2,1)S(1)}, u32[]{:S(2)}, u32[]{:S(2)}) %collective-permute-start.25) | collective-permute-done | bytes 147488 | tf_op jit(solution)/shard_map/ppermute | solution.py:544
  52.2 9.3 %collective-permute-done.28.theirs_ref = bf16[512,384]{1,0:T(8,128)(2,1)S(1)} collective-permute-done((bf16[512,384]{1,0:T(8,128)(2,1)S(1)}, bf16[512,384]{1,0:T(8,128)(2,1)S(1)}, u32[]{:S(2)}, u32[]{:S(2)}) %collective-permute-start.28) | collective-permute-done | bytes 393248 | tf_op jit(solution)/shard_map/ppermute | solution.py:635
  61.6 6.5 %feed.3 = (bf16[512,768]{1,0:T(8,128)(2,1)S(1)}, bf16[512,1536]{1,0:T(8,128)(2,1)S(1)}, bf16[512,1536]{1,0:T(8,128)(2,1)S(1)}, bf16[512,768]{1,0:T(8,128)(2,1)S(1)}) custom-call(s32[69]{0:T(128)S(1)} %copy-done.40, bf16[512,384]{1,0:T(8,128)(2,1)S(1)} %get-tuple-element.211.mine_ref, bf16[512,384]{1,0:T(8,128)(2,1)S(1)} %collective-permute-done.28.theirs_ref, ...), custom_call_target="tpu_custom_call" | custom-call | flops 7000000000 | bytes 1000 | tf_op jit(solution)/shard_map/feed/pallas_call | solution.py:66
  69.0 7.3 %feed.2 = (bf16[512,768]{1,0:T(8,128)(2,1)S(1)}, bf16[512,1536]{1,0:T(8,128)(2,1)S(1)}, bf16[512,1536]{1,0:T(8,128)(2,1)S(1)}, bf16[512,768]{1,0:T(8,128)(2,1)S(1)}, f32[512,768]{1,0:T(8,128)}) custom-call(s32[69]{0:T(128)S(1)} %copy-done.40, bf16[512,384]{1,0:T(8,128)(2,1)S(1)} %get-tuple-element.210.mine_ref, ...), custom_call_target="tpu_custom_call" | custom-call | flops 7000000000 | bytes 1000 | tf_op jit(solution)/shard_map/feed/pallas_call | solution.py:66
  76.3 7.9 %feed_grads.1 = (bf16[768,1536]{1,0:T(8,128)(2,1)}, bf16[1536,768]{1,0:T(8,128)(2,1)}, f32[1,1536]{1,0:T(1,128)}) custom-call(bf16[512,768]{1,0:T(8,128)(2,1)S(1)} %get-tuple-element.218.n_own, bf16[512,768]{1,0:T(8,128)(2,1)S(1)} %get-tuple-element.219.n_other, bf16[512,1536]{1,0:T(8,128)(2,1)S(1)} %get-tuple-element.220.a_own, ...), custom_call_target="tpu_custom_call" | custom-call | flops 300000000 | bytes 1000 | tf_op jit(solution)/shard_map/feed_grads/pallas_call | solution.py:66
  85.4 4.6 %middle.1 = (f32[512,768]{1,0:T(8,128)}, bf16[512,768]{1,0:T(8,128)(2,1)S(1)}, f32[4,768]{1,0:T(4,128)}) custom-call(bf16[512,768]{1,0:T(8,128)(2,1)S(1)} %get-tuple-element.214.mine_ref, bf16[512,768]{1,0:T(8,128)(2,1)S(1)} %collective-permute-done.29.got_ref, f32[512,768]{1,0:T(8,128)} %get-tuple-element.227.attn_ref, ...), custom_call_target="tpu_custom_call" | custom-call | flops 200000000 | bytes 1000 | tf_op jit(solution)/shard_map/middle/pallas_call | solution.py:66
  90.1 136.5 %conditional.1 = (bf16[512,768]{1,0:T(8,128)(2,1)S(1)}, f32[512,768]{1,0:T(8,128)}, f32[768]{0:T(1024)}, f32[768]{0:T(1024)}, f32[768]{0:T(1024)}, /*index=5*/f3...) conditional(s32[]{:T(128)} %convert_element_type.52, () %tuple.32, ...), branch_computations={%region_3.4_spmd, %region_4.7_spmd} | conditional | flops 30006243328 | bytes 103124904 | solution.py:871
  91.5 3.7 %branch.3 = bf16[512,768]{1,0:T(8,128)(2,1)S(1)} custom-call(bf16[512,1536]{1,0:T(8,128)(2,1)S(1)} %get-tuple-element.58.act_ref, bf16[1536,768]{1,0:T(8,128)(2,1)} %get-tuple-element.55.w2_ref), custom_call_target="tpu_custom_call" | custom-call | flops 2000000000 | bytes 1000 | tf_op jit(solution)/shard_map/cond/branch_1_fun/branch/pallas_call | solution.py:66
  97.3 13.4 %collective-permute-done.other_ref.g_other = bf16[512,768]{1,0:T(8,128)(2,1)S(1)} collective-permute-done((bf16[512,768]{1,0:T(8,128)(2,1)S(1)}, bf16[512,768]{1,0:T(8,128)(2,1)S(1)}, u32[]{:S(2)}, u32[]{:S(2)}) %collective-permute-start) | collective-permute-done | bytes 786464 | tf_op jit(solution)/shard_map/cond/branch_1_fun/ppermute | solution.py:635
  110.7 5.6 %attention_back.1.grad_ref = bf16[3,3,1280,128]{3,2,1,0:T(8,128)(2,1)S(1)} custom-call(s32[69]{0:T(128)S(1)} %get-tuple-element.51.meta, bf16[3,3,1280,128]{3,2,1,0:T(8,128)(2,1)S(1)} %copy-done.49, bf16[512,768]{1,0:T(8,128)(2,1)S(1)} %get-tuple-element.53.own_ref.g_own, bf16[512,768]{1,0:T(8,128)(2,1)S(1)} %collective-permute-done.other_ref.g_other, ...), custom_call_target="tpu_custom_call" | custom-call | flops 8999999488 | bytes 1000 | tf_op jit(solution)/shard_map/cond/branch_1_fun/attention_back/pallas_call | solution.py:66
  116.3 5.7 %collective-permute-done.1 = bf16[512,768]{1,0:T(8,128)(2,1)S(1)} collective-permute-done((bf16[512,768]{1,0:T(8,128)(2,1)S(1)}, bf16[512,768]{1,0:T(8,128)(2,1)S(1)}, u32[]{:S(2)}, u32[]{:S(2)}) %collective-permute-start.1) | collective-permute-done | bytes 786464 | tf_op jit(solution)/shard_map/cond/branch_1_fun/ppermute | solution.py:635
  122.0 2.4 weights_give.1
  130.0 3.7 %share.1 = (bf16[512,768]{1,0:T(8,128)(2,1)S(1)}, bf16[512,768]{1,0:T(8,128)(2,1)S(1)}) custom-call(s32[69]{0:T(128)S(1)} %get-tuple-element.51.meta, bf16[3,3,1280,128]{3,2,1,0:T(8,128)(2,1)S(1)} %attention_back.1.grad_ref, bf16[3,768,384]{2,1,0:T(8,128)(2,1)S(1)} %copy-done.47), custom_call_target="tpu_custom_call" | custom-call | flops 3000000000 | bytes 1000 | tf_op jit(solution)/shard_map/cond/branch_1_fun/share/pallas_call | solution.py:66
  136.3 12.2 %collective-permute-done.3.got_ref = bf16[768,384]{1,0:T(8,128)(2,1)S(1)} collective-permute-done((bf16[768,384]{1,0:T(8,128)(2,1)S(1)}, bf16[768,384]{1,0:T(8,128)(2,1)S(1)}, u32[]{:S(2)}, u32[]{:S(2)}) %collective-permute-start.3) | collective-permute-done | bytes 589856 | tf_op jit(solution)/shard_map/cond/branch_1_fun/ppermute | solution.py:544
  149.2 3.1 %collective-permute-start.4 = (bf16[384,384]{1,0:T(8,128)(2,1)S(1)}, bf16[384,384]{1,0:T(8,128)(2,1)S(1)}, u32[]{:S(2)}, u32[]{:S(2)}) collective-permute-start(bf16[384,384]{1,0:T(8,128)(2,1)S(1)} %get-tuple-element.87), channel_id=1, source_target_pairs={{0,8},{2,10},{4,12},{6,14},{8,0},{10,2},{12,4},{14,6},{16,24},{18,... | collective-permute-start | bytes 884744 | tf_op jit(solution)/shard_map/cond/branch_1_fun/ppermute | solution.py:544
  153.3 10.2 %collective-permute-done.4.got_ref = bf16[384,384]{1,0:T(8,128)(2,1)S(1)} collective-permute-done((bf16[384,384]{1,0:T(8,128)(2,1)S(1)}, bf16[384,384]{1,0:T(8,128)(2,1)S(1)}, u32[]{:S(2)}, u32[]{:S(2)}) %collective-permute-start.4) | collective-permute-done | bytes 294944 | tf_op jit(solution)/shard_map/cond/branch_1_fun/ppermute | solution.py:544
  164.3 4.2 %collective-permute-start.5 = (bf16[192,384]{1,0:T(8,128)(2,1)S(1)}, bf16[192,384]{1,0:T(8,128)(2,1)S(1)}, u32[]{:S(2)}, u32[]{:S(2)}) collective-permute-start(bf16[192,384]{1,0:T(8,128)(2,1)S(1)} %get-tuple-element.88), channel_id=1, source_target_pairs={{0,16},{2,18},{4,20},{6,22},{8,24},{10,26},{12,28},{14,30},{16,0},... | collective-permute-start | bytes 442376 | tf_op jit(solution)/shard_map/cond/branch_1_fun/ppermute | solution.py:544
  168.6 2.6 %final.1 = (f32[512,768]{1,0:T(8,128)}, f32[3,768]{1,0:T(4,128)S(1)}) custom-call(bf16[512,768]{1,0:T(8,128)(2,1)S(1)} %copy-done.3, bf16[512,768]{1,0:T(8,128)(2,1)S(1)} %collective-permute-done.6.got_ref, bf16[512,768]{1,0:T(8,128)(2,1)S(1)} %copy-done.11, f32[512,768]{1,0:T(8,128)S(1)} %copy-done.48, f32[512,1]{1,0:T(8,128)S(1)} %copy.42.mark_ref, ...), custom_call_target="tpu_custom_call" | custom-call | flops 3000000000 | bytes 1000 | tf_op jit(solution)/shard_map/cond/branch_1_fun/final/pallas_call | solution.py:66
  171.3 3.1 %collective-permute-done.5 = bf16[192,384]{1,0:T(8,128)(2,1)S(1)} collective-permute-done((bf16[192,384]{1,0:T(8,128)(2,1)S(1)}, bf16[192,384]{1,0:T(8,128)(2,1)S(1)}, u32[]{:S(2)}, u32[]{:S(2)}) %collective-permute-start.5) | collective-permute-done | bytes 147488 | tf_op jit(solution)/shard_map/cond/branch_1_fun/ppermute | solution.py:544
  174.8 2.7 %collective-permute-start.8 = (f32[12,768]{1,0:T(8,128)S(1)}, f32[12,768]{1,0:T(8,128)S(1)}, u32[]{:S(2)}, u32[]{:S(2)}) collective-permute-start(f32[12,768]{1,0:T(8,128)S(1)} %concatenate.9), channel_id=1, source_target_pairs={{0,16},{2,18},{4,20},{6,22},{8,24},{10,26},{12,28},{14,30},{16,0},... | collective-permute-start | bytes 110600 | tf_op jit(solution)/shard_map/cond/branch_1_fun/ppermute | solution.py:544
  177.5 7.6 %collective-permute-done.8 = f32[12,768]{1,0:T(8,128)S(1)} collective-permute-done((f32[12,768]{1,0:T(8,128)S(1)}, f32[12,768]{1,0:T(8,128)S(1)}, u32[]{:S(2)}, u32[]{:S(2)}) %collective-permute-start.8) | collective-permute-done | bytes 36896 | tf_op jit(solution)/shard_map/cond/branch_1_fun/ppermute | solution.py:544
  185.7 5.3 %collective-permute-start.10 = (bf16[384,384]{1,0:T(8,128)(2,1)S(1)}, bf16[384,384]{1,0:T(8,128)(2,1)S(1)}, u32[]{:S(2)}, u32[]{:S(2)}) collective-permute-start(bf16[384,384]{1,0:T(8,128)(2,1)S(1)} %gather.2.refs_0_), channel_id=1, source_target_pairs={{0,4},{2,6},{4,0},{6,2},{8,12},{10,14},{12,8},{14,10},{16,20},{18,... | collective-permute-start | bytes 884744 | tf_op jit(solution)/shard_map/cond/branch_1_fun/ppermute | solution.py:544
  193.1 15.7 %collective-permute-done.12 = f32[12,768]{1,0:T(8,128)S(1)} collective-permute-done((f32[12,768]{1,0:T(8,128)S(1)}, f32[12,768]{1,0:T(8,128)S(1)}, u32[]{:S(2)}, u32[]{:S(2)}) %collective-permute-start.12) | collective-permute-done | bytes 36896 | tf_op jit(solution)/shard_map/cond/branch_1_fun/ppermute | solution.py:544
  215.9 5.9 %collective-permute-done.13.refs_6_ = bf16[384,384]{1,0:T(8,128)(2,1)S(1)} collective-permute-done((bf16[384,384]{1,0:T(8,128)(2,1)S(1)}, bf16[384,384]{1,0:T(8,128)(2,1)S(1)}, u32[]{:S(2)}, u32[]{:S(2)}) %collective-permute-start.13) | collective-permute-done | bytes 294944 | tf_op jit(solution)/shard_map/cond/branch_1_fun/ppermute | solution.py:544
  223.4 3.2 %unpack.1 = (f32[3,768,384]{2,1,0:T(8,128)}, f32[384,768]{1,0:T(8,128)}, f32[768]{0:T(1024)}, f32[768]{0:T(1024)}, f32[768]{0:T(1024)}, /*index=5*/f32[768]{0:T(...) custom-call(s32[69]{0:T(128)S(1)} %copy-done.43, ...), custom_call_target="tpu_custom_call" | custom-call | flops 3000000000 | bytes 1000 | tf_op jit(solution)/shard_map/cond/branch_1_fun/unpack/pallas_call | solution.py:66
  226.6 4.8 %convert_element_type.56 = f32[768,1536]{1,0:T(8,128)} convert(bf16[768,1536]{1,0:T(8,128)(2,1)} %get-tuple-element.304) | non-fusion elementwise | flops 1179648 | bytes 7077888 | tf_op jit(solution)/shard_map/convert_element_type | solution.py:887
  231.5 2.5 %convert_element_type.57 = f32[1536,768]{1,0:T(8,128)} convert(bf16[1536,768]{1,0:T(8,128)(2,1)S(1)} %copy-done.12) | non-fusion elementwise | flops 1179648 | bytes 7077888 | tf_op jit(solution)/shard_map/convert_element_type | solution.py:889
  (194 shorter events, 44.7 us)
Async XLA Ops:
  7.2 219.4 %all-reduce.3.cloned.1.call-start = ((), (), s32[]{:S(2)}) async-start(), calls=%async_computation | async-start | bytes 9437184 | tf_op jit(solution)/shard_map/psum | solution.py:745
  7.2 19.1 %collective-permute-start.22 = (s32[512]{0:T(512)}, s32[512]{0:T(512)S(1)}, u32[]{:S(2)}, u32[]{:S(2)}) collective-permute-start(s32[512]{0:T(512)} %param.23), channel_id=1, source_target_pairs={{0,1},{1,0},{2,3},{3,2},{4,5},{5,4},{6,7},{7,6},{8,9},{9,8},{10,11... | collective-permute-start | bytes 6152 | tf_op jit(solution)/shard_map/ppermute | solution.py:635
  10.3 20.7 %collective-permute-start.21 = (bf16[512,768]{1,0:T(8,128)(2,1)}, bf16[512,768]{1,0:T(8,128)(2,1)S(1)}, u32[]{:S(2)}, u32[]{:S(2)}) collective-permute-start(bf16[512,768]{1,0:T(8,128)(2,1)} %tokens_ref.1), channel_id=1, source_target_pairs={{0,1},{1,0},{2,3},{3,2},{4,5},{5,4},{6,7},{7,6},{8,9},{9,8},{10,11... | collective-permute-start | bytes 2359304 | tf_op jit(solution)/shard_map/ppermute | solution.py:635
  20.0 19.5 %collective-permute-start.23 = (bf16[192,384]{1,0:T(8,128)(2,1)}, bf16[192,384]{1,0:T(8,128)(2,1)S(1)}, u32[]{:S(2)}, u32[]{:S(2)}) collective-permute-start(bf16[192,384]{1,0:T(8,128)(2,1)} %dynamic_slice.3), channel_id=1, source_target_pairs={{0,1},{1,0},{2,3},{3,2},{4,5},{5,4},{6,7},{7,6},{8,9},{9,8},{10,11... | collective-permute-start | bytes 442376 | tf_op jit(solution)/shard_map/ppermute | solution.py:604
  30.9 18.5 %collective-permute-start.24 = (bf16[512,768]{1,0:T(8,128)(2,1)S(1)}, bf16[512,768]{1,0:T(8,128)(2,1)S(1)}, u32[]{:S(2)}, u32[]{:S(2)}) collective-permute-start(bf16[512,768]{1,0:T(8,128)(2,1)S(1)} %get-tuple-element.208.gb_ref.g_own), channel_id=1, source_target_pairs={{0,1},{1,0},{2,3},{3,2},{4,5},{5,4},{6,7},{7,6},{8,9},{9,8},{10,11... | collective-permute-start | bytes 2359304 | tf_op jit(solution)/shard_map/ppermute | solution.py:635
  39.6 7.8 %collective-permute-start.25 = (bf16[192,384]{1,0:T(8,128)(2,1)S(1)}, bf16[192,384]{1,0:T(8,128)(2,1)S(1)}, u32[]{:S(2)}, u32[]{:S(2)}) collective-permute-start(bf16[192,384]{1,0:T(8,128)(2,1)S(1)} %collective-permute-done.23.refs_0_), channel_id=1, source_target_pairs={{0,4},{2,6},{4,0},{6,2},{8,12},{10,14},{12,8},{14,10},{16,20},{18,... | collective-permute-start | bytes 442376 | tf_op jit(solution)/shard_map/ppermute | solution.py:544
  49.5 12.1 %collective-permute-start.28 = (bf16[512,384]{1,0:T(8,128)(2,1)S(1)}, bf16[512,384]{1,0:T(8,128)(2,1)S(1)}, u32[]{:S(2)}, u32[]{:S(2)}) collective-permute-start(bf16[512,384]{1,0:T(8,128)(2,1)S(1)} %get-tuple-element.210.mine_ref), channel_id=1, source_target_pairs={{0,1},{1,0},{2,3},{3,2},{4,5},{5,4},{6,7},{7,6},{8,9},{9,8},{10,11... | collective-permute-start | bytes 1179656 | tf_op jit(solution)/shard_map/ppermute | solution.py:635
  50.5 1.8 collective-permute-start.27
  50.5 18.4 %collective-permute-start.26 = (bf16[512,384]{1,0:T(8,128)(2,1)S(1)}, bf16[512,384]{1,0:T(8,128)(2,1)S(1)}, u32[]{:S(2)}, u32[]{:S(2)}) collective-permute-start(bf16[512,384]{1,0:T(8,128)(2,1)S(1)} %get-tuple-element.211.mine_ref), channel_id=1, source_target_pairs={{0,1},{1,0},{2,3},{3,2},{4,5},{5,4},{6,7},{7,6},{8,9},{9,8},{10,11... | collective-permute-start | bytes 1179656 | tf_op jit(solution)/shard_map/ppermute | solution.py:635
  68.1 16.1 %collective-permute-start.29 = (bf16[512,768]{1,0:T(8,128)(2,1)S(1)}, bf16[512,768]{1,0:T(8,128)(2,1)S(1)}, u32[]{:S(2)}, u32[]{:S(2)}) collective-permute-start(bf16[512,768]{1,0:T(8,128)(2,1)S(1)} %get-tuple-element.217), channel_id=1, source_target_pairs={{0,1},{1,0},{2,3},{3,2},{4,5},{5,4},{6,7},{7,6},{8,9},{9,8},{10,11... | collective-permute-start | bytes 2359304 | tf_op jit(solution)/shard_map/ppermute | solution.py:635
  90.2 58.3 %copy-start.42 = (s32[69]{0:T(128)}, s32[69]{0:T(128)S(1)}, u32[]{:S(2)}) copy-start(s32[69]{0:T(128)S(1)} %get-tuple-element.51.meta) | copy-start | bytes 832 | tf_op jit(solution)/shard_map/cond
  90.2 20.5 %collective-permute-start = (bf16[512,768]{1,0:T(8,128)(2,1)S(1)}, bf16[512,768]{1,0:T(8,128)(2,1)S(1)}, u32[]{:S(2)}, u32[]{:S(2)}) collective-permute-start(bf16[512,768]{1,0:T(8,128)(2,1)S(1)} %get-tuple-element.53.own_ref.g_own), channel_id=1, source_target_pairs={{0,1},{1,0},{2,3},{3,2},{4,5},{5,4},{6,7},{7,6},{8,9},{9,8},{10,11... | collective-permute-start | bytes 2359304 | tf_op jit(solution)/shard_map/cond/branch_1_fun/ppermute | solution.py:635
  95.2 26.8 %collective-permute-start.1 = (bf16[512,768]{1,0:T(8,128)(2,1)S(1)}, bf16[512,768]{1,0:T(8,128)(2,1)S(1)}, u32[]{:S(2)}, u32[]{:S(2)}) collective-permute-start(bf16[512,768]{1,0:T(8,128)(2,1)S(1)} %branch.3), channel_id=1, source_target_pairs={{0,1},{1,0},{2,3},{3,2},{4,5},{5,4},{6,7},{7,6},{8,9},{9,8},{10,11... | collective-permute-start | bytes 2359304 | tf_op jit(solution)/shard_map/cond/branch_1_fun/ppermute | solution.py:635
  124.4 3.2 %collective-permute-start.2 = (bf16[1536,384]{1,0:T(8,128)(2,1)S(1)}, bf16[1536,384]{1,0:T(8,128)(2,1)S(1)}, u32[]{:S(2)}, u32[]{:S(2)}) collective-permute-start(bf16[1536,384]{1,0:T(8,128)(2,1)S(1)} %weights_give.1), channel_id=1, source_target_pairs={{0,2},{2,0},{4,6},{6,4},{8,10},{10,8},{12,14},{14,12},{16,18},{18,... | collective-permute-start | bytes 3538952 | tf_op jit(solution)/shard_map/cond/branch_1_fun/ppermute | solution.py:544
  128.5 20.0 %collective-permute-start.3 = (bf16[768,384]{1,0:T(8,128)(2,1)S(1)}, bf16[768,384]{1,0:T(8,128)(2,1)S(1)}, u32[]{:S(2)}, u32[]{:S(2)}) collective-permute-start(bf16[768,384]{1,0:T(8,128)(2,1)S(1)} %get-tuple-element.69), channel_id=1, source_target_pairs={{0,4},{2,6},{4,0},{6,2},{8,12},{10,14},{12,8},{14,10},{16,20},{18,... | collective-permute-start | bytes 1769480 | tf_op jit(solution)/shard_map/cond/branch_1_fun/ppermute | solution.py:544
  133.7 34.9 %collective-permute-start.6 = (bf16[512,768]{1,0:T(8,128)(2,1)S(1)}, bf16[512,768]{1,0:T(8,128)(2,1)S(1)}, u32[]{:S(2)}, u32[]{:S(2)}) collective-permute-start(bf16[512,768]{1,0:T(8,128)(2,1)S(1)} %get-tuple-element.91), channel_id=1, source_target_pairs={{0,1},{1,0},{2,3},{3,2},{4,5},{5,4},{6,7},{7,6},{8,9},{9,8},{10,11... | collective-permute-start | bytes 2359304 | tf_op jit(solution)/shard_map/cond/branch_1_fun/ppermute | solution.py:635
  149.2 14.3 %collective-permute-start.4 = (bf16[384,384]{1,0:T(8,128)(2,1)S(1)}, bf16[384,384]{1,0:T(8,128)(2,1)S(1)}, u32[]{:S(2)}, u32[]{:S(2)}) collective-permute-start(bf16[384,384]{1,0:T(8,128)(2,1)S(1)} %get-tuple-element.87), channel_id=1, source_target_pairs={{0,8},{2,10},{4,12},{6,14},{8,0},{10,2},{12,4},{14,6},{16,24},{18,... | collective-permute-start | bytes 884744 | tf_op jit(solution)/shard_map/cond/branch_1_fun/ppermute | solution.py:544
  164.3 10.1 %collective-permute-start.5 = (bf16[192,384]{1,0:T(8,128)(2,1)S(1)}, bf16[192,384]{1,0:T(8,128)(2,1)S(1)}, u32[]{:S(2)}, u32[]{:S(2)}) collective-permute-start(bf16[192,384]{1,0:T(8,128)(2,1)S(1)} %get-tuple-element.88), channel_id=1, source_target_pairs={{0,16},{2,18},{4,20},{6,22},{8,24},{10,26},{12,28},{14,30},{16,0},... | collective-permute-start | bytes 442376 | tf_op jit(solution)/shard_map/cond/branch_1_fun/ppermute | solution.py:544
  174.5 10.6 %collective-permute-start.7 = (bf16[192,384]{1,0:T(8,128)(2,1)S(1)}, bf16[192,384]{1,0:T(8,128)(2,1)S(1)}, u32[]{:S(2)}, u32[]{:S(2)}) collective-permute-start(bf16[192,384]{1,0:T(8,128)(2,1)S(1)} %add_convert_fusion.refs_0_), channel_id=1, source_target_pairs={{0,16},{2,18},{4,20},{6,22},{8,24},{10,26},{12,28},{14,30},{16,0},... | collective-permute-start | bytes 442376 | tf_op jit(solution)/shard_map/cond/branch_1_fun/ppermute | solution.py:544
  174.8 10.3 %collective-permute-start.8 = (f32[12,768]{1,0:T(8,128)S(1)}, f32[12,768]{1,0:T(8,128)S(1)}, u32[]{:S(2)}, u32[]{:S(2)}) collective-permute-start(f32[12,768]{1,0:T(8,128)S(1)} %concatenate.9), channel_id=1, source_target_pairs={{0,16},{2,18},{4,20},{6,22},{8,24},{10,26},{12,28},{14,30},{16,0},... | collective-permute-start | bytes 110600 | tf_op jit(solution)/shard_map/cond/branch_1_fun/ppermute | solution.py:544
  185.7 23.1 %collective-permute-start.11 = (bf16[384,384]{1,0:T(8,128)(2,1)S(1)}, bf16[384,384]{1,0:T(8,128)(2,1)S(1)}, u32[]{:S(2)}, u32[]{:S(2)}) collective-permute-start(bf16[384,384]{1,0:T(8,128)(2,1)S(1)} %gather.2.refs_0_), channel_id=1, source_target_pairs={{0,2},{2,0},{4,6},{6,4},{8,10},{10,8},{12,14},{14,12},{16,18},{18,... | collective-permute-start | bytes 884744 | tf_op jit(solution)/shard_map/cond/branch_1_fun/ppermute | solution.py:544
  185.7 23.0 %collective-permute-start.10 = (bf16[384,384]{1,0:T(8,128)(2,1)S(1)}, bf16[384,384]{1,0:T(8,128)(2,1)S(1)}, u32[]{:S(2)}, u32[]{:S(2)}) collective-permute-start(bf16[384,384]{1,0:T(8,128)(2,1)S(1)} %gather.2.refs_0_), channel_id=1, source_target_pairs={{0,4},{2,6},{4,0},{6,2},{8,12},{10,14},{12,8},{14,10},{16,20},{18,... | collective-permute-start | bytes 884744 | tf_op jit(solution)/shard_map/cond/branch_1_fun/ppermute | solution.py:544
  191.0 17.7 %collective-permute-start.9 = (bf16[384,384]{1,0:T(8,128)(2,1)S(1)}, bf16[384,384]{1,0:T(8,128)(2,1)S(1)}, u32[]{:S(2)}, u32[]{:S(2)}) collective-permute-start(bf16[384,384]{1,0:T(8,128)(2,1)S(1)} %gather.2.refs_0_), channel_id=1, source_target_pairs={{0,8},{2,10},{4,12},{6,14},{8,0},{10,2},{12,4},{14,6},{16,24},{18,... | collective-permute-start | bytes 884744 | tf_op jit(solution)/shard_map/cond/branch_1_fun/ppermute | solution.py:544
  191.0 17.7 %collective-permute-start.12 = (f32[12,768]{1,0:T(8,128)S(1)}, f32[12,768]{1,0:T(8,128)S(1)}, u32[]{:S(2)}, u32[]{:S(2)}) collective-permute-start(f32[12,768]{1,0:T(8,128)S(1)} %add.63), channel_id=1, source_target_pairs={{0,8},{2,10},{4,12},{6,14},{8,0},{10,2},{12,4},{14,6},{16,24},{18,... | collective-permute-start | bytes 110600 | tf_op jit(solution)/shard_map/cond/branch_1_fun/ppermute | solution.py:544
  208.8 5.5 %collective-permute-start.17 = (f32[9,768]{1,0:T(8,128)S(1)}, f32[9,768]{1,0:T(8,128)S(1)}, u32[]{:S(2)}, u32[]{:S(2)}) collective-permute-start(f32[9,768]{1,0:T(8,128)S(1)} %bitcast.8), channel_id=1, source_target_pairs={{0,5},{1,4},{2,7},{3,6},{4,1},{5,0},{6,3},{7,2},{8,13},{9,12},{10,... | collective-permute-start | bytes 82952 | tf_op jit(solution)/shard_map/cond/branch_1_fun/ppermute | solution.py:847
  209.6 4.7 %collective-permute-start.16 = (f32[9,768]{1,0:T(8,128)S(1)}, f32[9,768]{1,0:T(8,128)S(1)}, u32[]{:S(2)}, u32[]{:S(2)}) collective-permute-start(f32[9,768]{1,0:T(8,128)S(1)} %bitcast.9), channel_id=1, source_target_pairs={{0,1},{1,0},{2,3},{3,2},{4,5},{5,4},{6,7},{7,6},{8,9},{9,8},{10,11... | collective-permute-start | bytes 82952 | tf_op jit(solution)/shard_map/cond/branch_1_fun/ppermute | solution.py:635
  210.5 4.1 %collective-permute-start.18 = (f32[12,768]{1,0:T(8,128)S(1)}, f32[12,768]{1,0:T(8,128)S(1)}, u32[]{:S(2)}, u32[]{:S(2)}) collective-permute-start(f32[12,768]{1,0:T(8,128)S(1)} %add.64), channel_id=1, source_target_pairs={{0,4},{2,6},{4,0},{6,2},{8,12},{10,14},{12,8},{14,10},{16,20},{18,... | collective-permute-start | bytes 110600 | tf_op jit(solution)/shard_map/cond/branch_1_fun/ppermute | solution.py:544
  212.3 3.5 %collective-permute-start.14 = (bf16[384,384]{1,0:T(8,128)(2,1)S(1)}, bf16[384,384]{1,0:T(8,128)(2,1)S(1)}, u32[]{:S(2)}, u32[]{:S(2)}) collective-permute-start(bf16[384,384]{1,0:T(8,128)(2,1)S(1)} %collective-permute-done.9.refs_4_), channel_id=1, source_target_pairs={{0,2},{2,0},{4,6},{6,4},{8,10},{10,8},{12,14},{14,12},{16,18},{18,... | collective-permute-start | bytes 884744 | tf_op jit(solution)/shard_map/cond/branch_1_fun/ppermute | solution.py:544
  212.3 9.4 %collective-permute-start.13 = (bf16[384,384]{1,0:T(8,128)(2,1)S(1)}, bf16[384,384]{1,0:T(8,128)(2,1)S(1)}, u32[]{:S(2)}, u32[]{:S(2)}) collective-permute-start(bf16[384,384]{1,0:T(8,128)(2,1)S(1)} %collective-permute-done.9.refs_4_), channel_id=1, source_target_pairs={{0,4},{2,6},{4,0},{6,2},{8,12},{10,14},{12,8},{14,10},{16,20},{18,... | collective-permute-start | bytes 884744 | tf_op jit(solution)/shard_map/cond/branch_1_fun/ppermute | solution.py:544
  214.3 1.6 collective-permute-start.15
  221.8 1.7 collective-permute-start.20
  221.8 1.6 collective-permute-start.19
  (49 other events, 424.9 us)
Sparse Core Ops, SparseCore 0:
  84.4 135.5 all-reduce.2

commit v2 on v1

--- a/solution.py
+++ b/solution.py
@@ -19,6 +19,7 @@
 BF16 = jnp.bfloat16
 WINDOW = 256
 BIG_ROWS = 128
+MIX_ROWS = 144
 SWAP = ((0, 1), (1, 0))
 
 
@@ -225,11 +226,11 @@
         mask = lax.broadcasted_iota(jnp.int32, (1, B3), 1) < length
 
         def block(b, carry):
-            begin = pl.multiple_of(first + b * BIG_ROWS, 16)
-            mix(range(pairs), begin, BIG_ROWS, pl.ds(first, B3), mask)
+            begin = pl.multiple_of(first + b * MIX_ROWS, 16)
+            mix(range(pairs), begin, MIX_ROWS, pl.ds(first, B3), mask)
             return carry
 
-        lax.fori_loop(0, pl.cdiv(B3, BIG_ROWS), block, 0)
+        lax.fori_loop(0, pl.cdiv(B3, MIX_ROWS), block, 0)
 
     walk_groups(meta, slots, small, big)
     for p in range(pairs):

time: 242 us -> 241 us (level); the launches traced: 241 us -> 244 us
  waiting for transfers between devices: 97.5 us -> 84.9 us
  starting transfers between devices: 39.2 us -> 49.1 us
  Pallas kernels: 67.2 us -> 72.6 us
    ppermute x10, waiting for transfers between devices: 35.2 us -> 28.2 us  [shards(): swap = lambda v: lax.ppermute(v, 'narrow', SWAP)]
    pallas_call x19, Pallas kernels: 67.2 us -> 72.6 us  [call(): pl.pallas_call(kernel, out_shape=out_shape, grid_spec=spec, compiler_para...]
    ppermute x18, starting transfers between devices: 26.7 us -> 31.7 us  [hop(): lax.ppermute(value, 'wide', tuple(((i, i ^ flip) for i in range(size))))]
    ppermute x1, starting transfers between devices: 0.79 us -> 4.71 us  [rest(): lax.ppermute(small[:count], ('wide', 'narrow'), tuple(((i, i ^ flip) for...]
    ppermute x18, waiting for transfers between devices: 60.5 us -> 56.7 us  [hop(): lax.ppermute(value, 'wide', tuple(((i, i ^ flip) for i in range(size))))]
  transfers between devices with their start and end apart: 31 -> 31, of which waited for: 17 -> 15; matrix products, arithmetic and copies ran while one was open for 5% -> 5% of each run, Pallas kernels for 28% -> 30%
where the time goes in v2:
time: 241 us; the launch traced here: 244 us
  waiting for transfers between devices  84.9 us (35%)
  Pallas kernels  72.6 us (30%)
  starting transfers between devices  49.1 us (20%)
  between operations  15.1 us (6%)
  other arithmetic  14.3 us (6%)
  local copies, waits for them, and re-layouts  7.14 us (3%)
    pallas_call x19, Pallas kernels, call(): pl.pallas_call(kernel, out_shape=out_shape, grid_spec=spec, compiler_para...  72.6 us
    ppermute x18, waiting for transfers between devices, hop(): lax.ppermute(value, 'wide', tuple(((i, i ^ flip) for i in range(size))))  56.7 us
    ppermute x18, starting transfers between devices, hop(): lax.ppermute(value, 'wide', tuple(((i, i ^ flip) for i in range(size))))  31.7 us
    ppermute x10, waiting for transfers between devices, shards(): swap = lambda v: lax.ppermute(v, 'narrow', SWAP)  28.2 us
    ppermute x10, starting transfers between devices, shards(): swap = lambda v: lax.ppermute(v, 'narrow', SWAP)  10.7 us
  transfers between devices with their start and end apart: 31, of which 15 were waited for; matrix products, arithmetic and copies ran while one was open for 5% of the time, Pallas kernels for 30%

profile of v2, /device:TPU:0, one launch (start us, length us, event | category | flops | bytes accessed | tf_op | source)
XLA Modules:
  0.0 243.5 jit_solution(6946257144581701230)
XLA Ops:
  7.2 3.0 %collective-permute-start.22 = (s32[512]{0:T(512)}, s32[512]{0:T(512)S(1)}, u32[]{:S(2)}, u32[]{:S(2)}) collective-permute-start(s32[512]{0:T(512)} %param.23), channel_id=1, source_target_pairs={{0,1},{1,0},{2,3},{3,2},{4,5},{5,4},{6,7},{7,6},{8,9},{9,8},{10,11... | collective-permute-start | bytes 6152 | tf_op jit(solution)/shard_map/ppermute | solution.py:636
  14.8 3.6 %norm_qkv.1 = (bf16[512,768]{1,0:T(8,128)(2,1)}, bf16[3,3,512,128]{3,2,1,0:T(8,128)(2,1)S(1)}, bf16[512,768]{1,0:T(8,128)(2,1)}) custom-call(bf16[512,768]{1,0:T(8,128)(2,1)S(1)} %copy-done.1, f32[512,1]{1,0:T(8,128)S(1)} %copy.40.mark_ref, bf16[12,768]{1,0:T(8,128)(2,1)S(1)} %select_select_fusion.vec_ref, bf16[3,768,384]{2,1,0:T(8,128)(2,1)} %w_ref.3), custom_call_target="tpu_custom_call" | custom-call | flops 2000000000 | bytes 1000 | tf_op jit(solution)/shard_map/norm_qkv/pallas_call | solution.py:67
  20.0 1.9 collective-permute-start.23
  23.5 2.3 multiply_convert_fusion
  26.5 4.4 %collective-permute-done.21.tokens_ref = bf16[512,768]{1,0:T(8,128)(2,1)S(1)} collective-permute-done((bf16[512,768]{1,0:T(8,128)(2,1)}, bf16[512,768]{1,0:T(8,128)(2,1)S(1)}, u32[]{:S(2)}, u32[]{:S(2)}) %collective-permute-start.21) | collective-permute-done | bytes 786464 | tf_op jit(solution)/shard_map/ppermute | solution.py:636
  31.0 10.4 %attention.1 = (bf16[512,384]{1,0:T(8,128)(2,1)S(1)}, bf16[512,384]{1,0:T(8,128)(2,1)S(1)}, bf16[3,3,1280,128]{3,2,1,0:T(8,128)(2,1)}, bf16[512,768]{1,0:T(8,128)(2,1)}, bf16[512,768]{1,0:T(8,128)(2,1)S(1)}) custom-call(s32[69]{0:T(128)} %concatenate.12.meta, bf16[3,3,512,128]{3,2,1,0:T(8,128)(2,1)S(1)} %get-tuple-element.200.own_ref, ...), custom_call_target="tpu_custom_call" | custom-call | flops 12000000000 | bytes 1000 | tf_op jit(solution)/shard_map/attention/pallas_call | solution.py:67
  41.4 5.3 %collective-permute-start.25 = (bf16[192,384]{1,0:T(8,128)(2,1)S(1)}, bf16[192,384]{1,0:T(8,128)(2,1)S(1)}, u32[]{:S(2)}, u32[]{:S(2)}) collective-permute-start(bf16[192,384]{1,0:T(8,128)(2,1)S(1)} %collective-permute-done.23.refs_0_), channel_id=1, source_target_pairs={{0,4},{2,6},{4,0},{6,2},{8,12},{10,14},{12,8},{14,10},{16,20},{18,... | collective-permute-start | bytes 442376 | tf_op jit(solution)/shard_map/ppermute | solution.py:545
  46.7 3.1 %collective-permute-done.25.refs_1_ = bf16[192,384]{1,0:T(8,128)(2,1)S(1)} collective-permute-done((bf16[192,384]{1,0:T(8,128)(2,1)S(1)}, bf16[192,384]{1,0:T(8,128)(2,1)S(1)}, u32[]{:S(2)}, u32[]{:S(2)}) %collective-permute-start.25) | collective-permute-done | bytes 147488 | tf_op jit(solution)/shard_map/ppermute | solution.py:545
  53.6 8.3 %collective-permute-done.28.theirs_ref = bf16[512,384]{1,0:T(8,128)(2,1)S(1)} collective-permute-done((bf16[512,384]{1,0:T(8,128)(2,1)S(1)}, bf16[512,384]{1,0:T(8,128)(2,1)S(1)}, u32[]{:S(2)}, u32[]{:S(2)}) %collective-permute-start.28) | collective-permute-done | bytes 393248 | tf_op jit(solution)/shard_map/ppermute | solution.py:636
  61.9 6.5 %feed.3 = (bf16[512,768]{1,0:T(8,128)(2,1)S(1)}, bf16[512,1536]{1,0:T(8,128)(2,1)S(1)}, bf16[512,1536]{1,0:T(8,128)(2,1)S(1)}, bf16[512,768]{1,0:T(8,128)(2,1)S(1)}) custom-call(s32[69]{0:T(128)S(1)} %copy-done.40, bf16[512,384]{1,0:T(8,128)(2,1)S(1)} %get-tuple-element.211.mine_ref, bf16[512,384]{1,0:T(8,128)(2,1)S(1)} %collective-permute-done.28.theirs_ref, ...), custom_call_target="tpu_custom_call" | custom-call | flops 7000000000 | bytes 1000 | tf_op jit(solution)/shard_map/feed/pallas_call | solution.py:67
  69.9 7.3 %feed.2 = (bf16[512,768]{1,0:T(8,128)(2,1)S(1)}, bf16[512,1536]{1,0:T(8,128)(2,1)S(1)}, bf16[512,1536]{1,0:T(8,128)(2,1)S(1)}, bf16[512,768]{1,0:T(8,128)(2,1)S(1)}, f32[512,768]{1,0:T(8,128)}) custom-call(s32[69]{0:T(128)S(1)} %copy-done.40, bf16[512,384]{1,0:T(8,128)(2,1)S(1)} %get-tuple-element.210.mine_ref, ...), custom_call_target="tpu_custom_call" | custom-call | flops 7000000000 | bytes 1000 | tf_op jit(solution)/shard_map/feed/pallas_call | solution.py:67
  77.2 7.9 %feed_grads.1 = (bf16[768,1536]{1,0:T(8,128)(2,1)}, bf16[1536,768]{1,0:T(8,128)(2,1)}, f32[1,1536]{1,0:T(1,128)}) custom-call(bf16[512,768]{1,0:T(8,128)(2,1)S(1)} %get-tuple-element.218.n_own, bf16[512,768]{1,0:T(8,128)(2,1)S(1)} %get-tuple-element.219.n_other, bf16[512,1536]{1,0:T(8,128)(2,1)S(1)} %get-tuple-element.220.a_own, ...), custom_call_target="tpu_custom_call" | custom-call | flops 300000000 | bytes 1000 | tf_op jit(solution)/shard_map/feed_grads/pallas_call | solution.py:67
  86.4 4.6 %middle.1 = (f32[512,768]{1,0:T(8,128)}, bf16[512,768]{1,0:T(8,128)(2,1)S(1)}, f32[4,768]{1,0:T(4,128)}) custom-call(bf16[512,768]{1,0:T(8,128)(2,1)S(1)} %get-tuple-element.214.mine_ref, bf16[512,768]{1,0:T(8,128)(2,1)S(1)} %collective-permute-done.29.got_ref, f32[512,768]{1,0:T(8,128)} %get-tuple-element.227.attn_ref, ...), custom_call_target="tpu_custom_call" | custom-call | flops 200000000 | bytes 1000 | tf_op jit(solution)/shard_map/middle/pallas_call | solution.py:67
  91.0 138.2 %conditional.1 = (bf16[512,768]{1,0:T(8,128)(2,1)S(1)}, f32[512,768]{1,0:T(8,128)}, f32[768]{0:T(1024)}, f32[768]{0:T(1024)}, f32[768]{0:T(1024)}, /*index=5*/f3...) conditional(s32[]{:T(128)} %convert_element_type.52, () %tuple.32, ...), branch_computations={%region_3.4_spmd, %region_4.7_spmd} | conditional | flops 30006243328 | bytes 103124904 | solution.py:872
  91.9 3.5 %branch.3 = bf16[512,768]{1,0:T(8,128)(2,1)S(1)} custom-call(bf16[512,1536]{1,0:T(8,128)(2,1)S(1)} %get-tuple-element.58.act_ref, bf16[1536,768]{1,0:T(8,128)(2,1)} %get-tuple-element.55.w2_ref), custom_call_target="tpu_custom_call" | custom-call | flops 2000000000 | bytes 1000 | tf_op jit(solution)/shard_map/cond/branch_1_fun/branch/pallas_call | solution.py:67
  98.6 13.1 %collective-permute-done.other_ref.g_other = bf16[512,768]{1,0:T(8,128)(2,1)S(1)} collective-permute-done((bf16[512,768]{1,0:T(8,128)(2,1)S(1)}, bf16[512,768]{1,0:T(8,128)(2,1)S(1)}, u32[]{:S(2)}, u32[]{:S(2)}) %collective-permute-start) | collective-permute-done | bytes 786464 | tf_op jit(solution)/shard_map/cond/branch_1_fun/ppermute | solution.py:636
  111.7 9.3 %attention_back.1.grad_ref = bf16[3,3,1280,128]{3,2,1,0:T(8,128)(2,1)S(1)} custom-call(s32[69]{0:T(128)S(1)} %get-tuple-element.51.meta, bf16[3,3,1280,128]{3,2,1,0:T(8,128)(2,1)S(1)} %copy-done.49, bf16[512,768]{1,0:T(8,128)(2,1)S(1)} %get-tuple-element.53.own_ref.g_own, bf16[512,768]{1,0:T(8,128)(2,1)S(1)} %collective-permute-done.other_ref.g_other, ...), custom_call_target="tpu_custom_call" | custom-call | flops 8999999488 | bytes 1000 | tf_op jit(solution)/shard_map/cond/branch_1_fun/attention_back/pallas_call | solution.py:67
  121.6 2.4 weights_give.1
  124.8 2.4 weights_keep.1
  128.1 7.2 %collective-permute-start.3 = (bf16[768,384]{1,0:T(8,128)(2,1)S(1)}, bf16[768,384]{1,0:T(8,128)(2,1)S(1)}, u32[]{:S(2)}, u32[]{:S(2)}) collective-permute-start(bf16[768,384]{1,0:T(8,128)(2,1)S(1)} %get-tuple-element.69), channel_id=1, source_target_pairs={{0,4},{2,6},{4,0},{6,2},{8,12},{10,14},{12,8},{14,10},{16,20},{18,... | collective-permute-start | bytes 1769480 | tf_op jit(solution)/shard_map/cond/branch_1_fun/ppermute | solution.py:545
  135.3 3.7 %share.1 = (bf16[512,768]{1,0:T(8,128)(2,1)S(1)}, bf16[512,768]{1,0:T(8,128)(2,1)S(1)}) custom-call(s32[69]{0:T(128)S(1)} %get-tuple-element.51.meta, bf16[3,3,1280,128]{3,2,1,0:T(8,128)(2,1)S(1)} %attention_back.1.grad_ref, bf16[3,768,384]{2,1,0:T(8,128)(2,1)S(1)} %copy-done.47), custom_call_target="tpu_custom_call" | custom-call | flops 3000000000 | bytes 1000 | tf_op jit(solution)/shard_map/cond/branch_1_fun/share/pallas_call | solution.py:67
  142.0 7.3 %collective-permute-done.3.got_ref = bf16[768,384]{1,0:T(8,128)(2,1)S(1)} collective-permute-done((bf16[768,384]{1,0:T(8,128)(2,1)S(1)}, bf16[768,384]{1,0:T(8,128)(2,1)S(1)}, u32[]{:S(2)}, u32[]{:S(2)}) %collective-permute-start.3) | collective-permute-done | bytes 589856 | tf_op jit(solution)/shard_map/cond/branch_1_fun/ppermute | solution.py:545
  151.8 9.1 %collective-permute-done.4.got_ref = bf16[384,384]{1,0:T(8,128)(2,1)S(1)} collective-permute-done((bf16[384,384]{1,0:T(8,128)(2,1)S(1)}, bf16[384,384]{1,0:T(8,128)(2,1)S(1)}, u32[]{:S(2)}, u32[]{:S(2)}) %collective-permute-start.4) | collective-permute-done | bytes 294944 | tf_op jit(solution)/shard_map/cond/branch_1_fun/ppermute | solution.py:545
  161.8 9.9 %collective-permute-start.5 = (bf16[192,384]{1,0:T(8,128)(2,1)S(1)}, bf16[192,384]{1,0:T(8,128)(2,1)S(1)}, u32[]{:S(2)}, u32[]{:S(2)}) collective-permute-start(bf16[192,384]{1,0:T(8,128)(2,1)S(1)} %get-tuple-element.88), channel_id=1, source_target_pairs={{0,16},{2,18},{4,20},{6,22},{8,24},{10,26},{12,28},{14,30},{16,0},... | collective-permute-start | bytes 442376 | tf_op jit(solution)/shard_map/cond/branch_1_fun/ppermute | solution.py:545
  171.8 2.6 %final.1 = (f32[512,768]{1,0:T(8,128)}, f32[3,768]{1,0:T(4,128)S(1)}) custom-call(bf16[512,768]{1,0:T(8,128)(2,1)S(1)} %copy-done.3, bf16[512,768]{1,0:T(8,128)(2,1)S(1)} %collective-permute-done.6.got_ref, bf16[512,768]{1,0:T(8,128)(2,1)S(1)} %copy-done.11, f32[512,768]{1,0:T(8,128)S(1)} %copy-done.48, f32[512,1]{1,0:T(8,128)S(1)} %copy.42.mark_ref, ...), custom_call_target="tpu_custom_call" | custom-call | flops 3000000000 | bytes 1000 | tf_op jit(solution)/shard_map/cond/branch_1_fun/final/pallas_call | solution.py:67
  179.3 11.2 %collective-permute-done.8 = f32[12,768]{1,0:T(8,128)S(1)} collective-permute-done((f32[12,768]{1,0:T(8,128)S(1)}, f32[12,768]{1,0:T(8,128)S(1)}, u32[]{:S(2)}, u32[]{:S(2)}) %collective-permute-start.8) | collective-permute-done | bytes 36896 | tf_op jit(solution)/shard_map/cond/branch_1_fun/ppermute | solution.py:545
  193.6 15.6 %collective-permute-done.12 = f32[12,768]{1,0:T(8,128)S(1)} collective-permute-done((f32[12,768]{1,0:T(8,128)S(1)}, f32[12,768]{1,0:T(8,128)S(1)}, u32[]{:S(2)}, u32[]{:S(2)}) %collective-permute-start.12) | collective-permute-done | bytes 36896 | tf_op jit(solution)/shard_map/cond/branch_1_fun/ppermute | solution.py:545
  209.2 4.7 %collective-permute-start.17 = (f32[9,768]{1,0:T(8,128)S(1)}, f32[9,768]{1,0:T(8,128)S(1)}, u32[]{:S(2)}, u32[]{:S(2)}) collective-permute-start(f32[9,768]{1,0:T(8,128)S(1)} %bitcast.8), channel_id=1, source_target_pairs={{0,5},{1,4},{2,7},{3,6},{4,1},{5,0},{6,3},{7,2},{8,13},{9,12},{10,... | collective-permute-start | bytes 82952 | tf_op jit(solution)/shard_map/cond/branch_1_fun/ppermute | solution.py:848
  218.5 5.9 %collective-permute-done.13.refs_6_ = bf16[384,384]{1,0:T(8,128)(2,1)S(1)} collective-permute-done((bf16[384,384]{1,0:T(8,128)(2,1)S(1)}, bf16[384,384]{1,0:T(8,128)(2,1)S(1)}, u32[]{:S(2)}, u32[]{:S(2)}) %collective-permute-start.13) | collective-permute-done | bytes 294944 | tf_op jit(solution)/shard_map/cond/branch_1_fun/ppermute | solution.py:545
  226.1 3.2 %unpack.1 = (f32[3,768,384]{2,1,0:T(8,128)}, f32[384,768]{1,0:T(8,128)}, f32[768]{0:T(1024)}, f32[768]{0:T(1024)}, f32[768]{0:T(1024)}, /*index=5*/f32[768]{0:T(...) custom-call(s32[69]{0:T(128)S(1)} %copy-done.43, ...), custom_call_target="tpu_custom_call" | custom-call | flops 3000000000 | bytes 1000 | tf_op jit(solution)/shard_map/cond/branch_1_fun/unpack/pallas_call | solution.py:67
  229.3 4.8 %convert_element_type.56 = f32[768,1536]{1,0:T(8,128)} convert(bf16[768,1536]{1,0:T(8,128)(2,1)} %get-tuple-element.304) | non-fusion elementwise | flops 1179648 | bytes 7077888 | tf_op jit(solution)/shard_map/convert_element_type | solution.py:888
  234.1 2.5 %convert_element_type.57 = f32[1536,768]{1,0:T(8,128)} convert(bf16[1536,768]{1,0:T(8,128)(2,1)S(1)} %copy-done.12) | non-fusion elementwise | flops 1179648 | bytes 7077888 | tf_op jit(solution)/shard_map/convert_element_type | solution.py:890
  (194 shorter events, 40.7 us)
Async XLA Ops:
  7.2 222.1 %all-reduce.3.cloned.1.call-start = ((), (), s32[]{:S(2)}) async-start(), calls=%async_computation | async-start | bytes 9437184 | tf_op jit(solution)/shard_map/psum | solution.py:746
  7.2 19.1 %collective-permute-start.22 = (s32[512]{0:T(512)}, s32[512]{0:T(512)S(1)}, u32[]{:S(2)}, u32[]{:S(2)}) collective-permute-start(s32[512]{0:T(512)} %param.23), channel_id=1, source_target_pairs={{0,1},{1,0},{2,3},{3,2},{4,5},{5,4},{6,7},{7,6},{8,9},{9,8},{10,11... | collective-permute-start | bytes 6152 | tf_op jit(solution)/shard_map/ppermute | solution.py:636
  10.3 20.7 %collective-permute-start.21 = (bf16[512,768]{1,0:T(8,128)(2,1)}, bf16[512,768]{1,0:T(8,128)(2,1)S(1)}, u32[]{:S(2)}, u32[]{:S(2)}) collective-permute-start(bf16[512,768]{1,0:T(8,128)(2,1)} %tokens_ref.1), channel_id=1, source_target_pairs={{0,1},{1,0},{2,3},{3,2},{4,5},{5,4},{6,7},{7,6},{8,9},{9,8},{10,11... | collective-permute-start | bytes 2359304 | tf_op jit(solution)/shard_map/ppermute | solution.py:636
  20.0 21.3 %collective-permute-start.23 = (bf16[192,384]{1,0:T(8,128)(2,1)}, bf16[192,384]{1,0:T(8,128)(2,1)S(1)}, u32[]{:S(2)}, u32[]{:S(2)}) collective-permute-start(bf16[192,384]{1,0:T(8,128)(2,1)} %dynamic_slice.3), channel_id=1, source_target_pairs={{0,1},{1,0},{2,3},{3,2},{4,5},{5,4},{6,7},{7,6},{8,9},{9,8},{10,11... | collective-permute-start | bytes 442376 | tf_op jit(solution)/shard_map/ppermute | solution.py:605
  30.9 18.9 %collective-permute-start.24 = (bf16[512,768]{1,0:T(8,128)(2,1)S(1)}, bf16[512,768]{1,0:T(8,128)(2,1)S(1)}, u32[]{:S(2)}, u32[]{:S(2)}) collective-permute-start(bf16[512,768]{1,0:T(8,128)(2,1)S(1)} %get-tuple-element.208.gb_ref.g_own), channel_id=1, source_target_pairs={{0,1},{1,0},{2,3},{3,2},{4,5},{5,4},{6,7},{7,6},{8,9},{9,8},{10,11... | collective-permute-start | bytes 2359304 | tf_op jit(solution)/shard_map/ppermute | solution.py:636
  41.4 8.4 %collective-permute-start.25 = (bf16[192,384]{1,0:T(8,128)(2,1)S(1)}, bf16[192,384]{1,0:T(8,128)(2,1)S(1)}, u32[]{:S(2)}, u32[]{:S(2)}) collective-permute-start(bf16[192,384]{1,0:T(8,128)(2,1)S(1)} %collective-permute-done.23.refs_0_), channel_id=1, source_target_pairs={{0,4},{2,6},{4,0},{6,2},{8,12},{10,14},{12,8},{14,10},{16,20},{18,... | collective-permute-start | bytes 442376 | tf_op jit(solution)/shard_map/ppermute | solution.py:545
  49.8 12.1 %collective-permute-start.28 = (bf16[512,384]{1,0:T(8,128)(2,1)S(1)}, bf16[512,384]{1,0:T(8,128)(2,1)S(1)}, u32[]{:S(2)}, u32[]{:S(2)}) collective-permute-start(bf16[512,384]{1,0:T(8,128)(2,1)S(1)} %get-tuple-element.210.mine_ref), channel_id=1, source_target_pairs={{0,1},{1,0},{2,3},{3,2},{4,5},{5,4},{6,7},{7,6},{8,9},{9,8},{10,11... | collective-permute-start | bytes 1179656 | tf_op jit(solution)/shard_map/ppermute | solution.py:636
  51.9 1.6 collective-permute-start.27
  52.0 17.9 %collective-permute-start.26 = (bf16[512,384]{1,0:T(8,128)(2,1)S(1)}, bf16[512,384]{1,0:T(8,128)(2,1)S(1)}, u32[]{:S(2)}, u32[]{:S(2)}) collective-permute-start(bf16[512,384]{1,0:T(8,128)(2,1)S(1)} %get-tuple-element.211.mine_ref), channel_id=1, source_target_pairs={{0,1},{1,0},{2,3},{3,2},{4,5},{5,4},{6,7},{7,6},{8,9},{9,8},{10,11... | collective-permute-start | bytes 1179656 | tf_op jit(solution)/shard_map/ppermute | solution.py:636
  68.5 16.6 %collective-permute-start.29 = (bf16[512,768]{1,0:T(8,128)(2,1)S(1)}, bf16[512,768]{1,0:T(8,128)(2,1)S(1)}, u32[]{:S(2)}, u32[]{:S(2)}) collective-permute-start(bf16[512,768]{1,0:T(8,128)(2,1)S(1)} %get-tuple-element.217), channel_id=1, source_target_pairs={{0,1},{1,0},{2,3},{3,2},{4,5},{5,4},{6,7},{7,6},{8,9},{9,8},{10,11... | collective-permute-start | bytes 2359304 | tf_op jit(solution)/shard_map/ppermute | solution.py:636
  91.1 58.2 %copy-start.42 = (s32[69]{0:T(128)}, s32[69]{0:T(128)S(1)}, u32[]{:S(2)}) copy-start(s32[69]{0:T(128)S(1)} %get-tuple-element.51.meta) | copy-start | bytes 832 | tf_op jit(solution)/shard_map/cond
  91.1 20.5 %collective-permute-start = (bf16[512,768]{1,0:T(8,128)(2,1)S(1)}, bf16[512,768]{1,0:T(8,128)(2,1)S(1)}, u32[]{:S(2)}, u32[]{:S(2)}) collective-permute-start(bf16[512,768]{1,0:T(8,128)(2,1)S(1)} %get-tuple-element.53.own_ref.g_own), channel_id=1, source_target_pairs={{0,1},{1,0},{2,3},{3,2},{4,5},{5,4},{6,7},{7,6},{8,9},{9,8},{10,11... | collective-permute-start | bytes 2359304 | tf_op jit(solution)/shard_map/cond/branch_1_fun/ppermute | solution.py:636
  95.4 26.2 %collective-permute-start.1 = (bf16[512,768]{1,0:T(8,128)(2,1)S(1)}, bf16[512,768]{1,0:T(8,128)(2,1)S(1)}, u32[]{:S(2)}, u32[]{:S(2)}) collective-permute-start(bf16[512,768]{1,0:T(8,128)(2,1)S(1)} %branch.3), channel_id=1, source_target_pairs={{0,1},{1,0},{2,3},{3,2},{4,5},{5,4},{6,7},{7,6},{8,9},{9,8},{10,11... | collective-permute-start | bytes 2359304 | tf_op jit(solution)/shard_map/cond/branch_1_fun/ppermute | solution.py:636
  124.0 3.2 %collective-permute-start.2 = (bf16[1536,384]{1,0:T(8,128)(2,1)S(1)}, bf16[1536,384]{1,0:T(8,128)(2,1)S(1)}, u32[]{:S(2)}, u32[]{:S(2)}) collective-permute-start(bf16[1536,384]{1,0:T(8,128)(2,1)S(1)} %weights_give.1), channel_id=1, source_target_pairs={{0,2},{2,0},{4,6},{6,4},{8,10},{10,8},{12,14},{14,12},{16,18},{18,... | collective-permute-start | bytes 3538952 | tf_op jit(solution)/shard_map/cond/branch_1_fun/ppermute | solution.py:545
  128.1 21.2 %collective-permute-start.3 = (bf16[768,384]{1,0:T(8,128)(2,1)S(1)}, bf16[768,384]{1,0:T(8,128)(2,1)S(1)}, u32[]{:S(2)}, u32[]{:S(2)}) collective-permute-start(bf16[768,384]{1,0:T(8,128)(2,1)S(1)} %get-tuple-element.69), channel_id=1, source_target_pairs={{0,4},{2,6},{4,0},{6,2},{8,12},{10,14},{12,8},{14,10},{16,20},{18,... | collective-permute-start | bytes 1769480 | tf_op jit(solution)/shard_map/cond/branch_1_fun/ppermute | solution.py:545
  139.1 32.7 %collective-permute-start.6 = (bf16[512,768]{1,0:T(8,128)(2,1)S(1)}, bf16[512,768]{1,0:T(8,128)(2,1)S(1)}, u32[]{:S(2)}, u32[]{:S(2)}) collective-permute-start(bf16[512,768]{1,0:T(8,128)(2,1)S(1)} %get-tuple-element.91), channel_id=1, source_target_pairs={{0,1},{1,0},{2,3},{3,2},{4,5},{5,4},{6,7},{7,6},{8,9},{9,8},{10,11... | collective-permute-start | bytes 2359304 | tf_op jit(solution)/shard_map/cond/branch_1_fun/ppermute | solution.py:636
  150.0 10.9 %collective-permute-start.4 = (bf16[384,384]{1,0:T(8,128)(2,1)S(1)}, bf16[384,384]{1,0:T(8,128)(2,1)S(1)}, u32[]{:S(2)}, u32[]{:S(2)}) collective-permute-start(bf16[384,384]{1,0:T(8,128)(2,1)S(1)} %get-tuple-element.87), channel_id=1, source_target_pairs={{0,8},{2,10},{4,12},{6,14},{8,0},{10,2},{12,4},{14,6},{16,24},{18,... | collective-permute-start | bytes 884744 | tf_op jit(solution)/shard_map/cond/branch_1_fun/ppermute | solution.py:545
  161.8 14.5 %collective-permute-start.5 = (bf16[192,384]{1,0:T(8,128)(2,1)S(1)}, bf16[192,384]{1,0:T(8,128)(2,1)S(1)}, u32[]{:S(2)}, u32[]{:S(2)}) collective-permute-start(bf16[192,384]{1,0:T(8,128)(2,1)S(1)} %get-tuple-element.88), channel_id=1, source_target_pairs={{0,16},{2,18},{4,20},{6,22},{8,24},{10,26},{12,28},{14,30},{16,0},... | collective-permute-start | bytes 442376 | tf_op jit(solution)/shard_map/cond/branch_1_fun/ppermute | solution.py:545
  176.3 14.2 %collective-permute-start.7 = (bf16[192,384]{1,0:T(8,128)(2,1)S(1)}, bf16[192,384]{1,0:T(8,128)(2,1)S(1)}, u32[]{:S(2)}, u32[]{:S(2)}) collective-permute-start(bf16[192,384]{1,0:T(8,128)(2,1)S(1)} %add_convert_fusion.refs_0_), channel_id=1, source_target_pairs={{0,16},{2,18},{4,20},{6,22},{8,24},{10,26},{12,28},{14,30},{16,0},... | collective-permute-start | bytes 442376 | tf_op jit(solution)/shard_map/cond/branch_1_fun/ppermute | solution.py:545
  178.0 12.5 %collective-permute-start.8 = (f32[12,768]{1,0:T(8,128)S(1)}, f32[12,768]{1,0:T(8,128)S(1)}, u32[]{:S(2)}, u32[]{:S(2)}) collective-permute-start(f32[12,768]{1,0:T(8,128)S(1)} %concatenate.9), channel_id=1, source_target_pairs={{0,16},{2,18},{4,20},{6,22},{8,24},{10,26},{12,28},{14,30},{16,0},... | collective-permute-start | bytes 110600 | tf_op jit(solution)/shard_map/cond/branch_1_fun/ppermute | solution.py:545
  191.1 18.1 %collective-permute-start.11 = (bf16[384,384]{1,0:T(8,128)(2,1)S(1)}, bf16[384,384]{1,0:T(8,128)(2,1)S(1)}, u32[]{:S(2)}, u32[]{:S(2)}) collective-permute-start(bf16[384,384]{1,0:T(8,128)(2,1)S(1)} %gather.2.refs_0_), channel_id=1, source_target_pairs={{0,2},{2,0},{4,6},{6,4},{8,10},{10,8},{12,14},{14,12},{16,18},{18,... | collective-permute-start | bytes 884744 | tf_op jit(solution)/shard_map/cond/branch_1_fun/ppermute | solution.py:545
  191.2 18.0 %collective-permute-start.10 = (bf16[384,384]{1,0:T(8,128)(2,1)S(1)}, bf16[384,384]{1,0:T(8,128)(2,1)S(1)}, u32[]{:S(2)}, u32[]{:S(2)}) collective-permute-start(bf16[384,384]{1,0:T(8,128)(2,1)S(1)} %gather.2.refs_0_), channel_id=1, source_target_pairs={{0,4},{2,6},{4,0},{6,2},{8,12},{10,14},{12,8},{14,10},{16,20},{18,... | collective-permute-start | bytes 884744 | tf_op jit(solution)/shard_map/cond/branch_1_fun/ppermute | solution.py:545
  191.5 17.7 %collective-permute-start.9 = (bf16[384,384]{1,0:T(8,128)(2,1)S(1)}, bf16[384,384]{1,0:T(8,128)(2,1)S(1)}, u32[]{:S(2)}, u32[]{:S(2)}) collective-permute-start(bf16[384,384]{1,0:T(8,128)(2,1)S(1)} %gather.2.refs_0_), channel_id=1, source_target_pairs={{0,8},{2,10},{4,12},{6,14},{8,0},{10,2},{12,4},{14,6},{16,24},{18,... | collective-permute-start | bytes 884744 | tf_op jit(solution)/shard_map/cond/branch_1_fun/ppermute | solution.py:545
  192.0 17.2 %collective-permute-start.12 = (f32[12,768]{1,0:T(8,128)S(1)}, f32[12,768]{1,0:T(8,128)S(1)}, u32[]{:S(2)}, u32[]{:S(2)}) collective-permute-start(f32[12,768]{1,0:T(8,128)S(1)} %add.63), channel_id=1, source_target_pairs={{0,8},{2,10},{4,12},{6,14},{8,0},{10,2},{12,4},{14,6},{16,24},{18,... | collective-permute-start | bytes 110600 | tf_op jit(solution)/shard_map/cond/branch_1_fun/ppermute | solution.py:545
  209.2 6.8 %collective-permute-start.17 = (f32[9,768]{1,0:T(8,128)S(1)}, f32[9,768]{1,0:T(8,128)S(1)}, u32[]{:S(2)}, u32[]{:S(2)}) collective-permute-start(f32[9,768]{1,0:T(8,128)S(1)} %bitcast.8), channel_id=1, source_target_pairs={{0,5},{1,4},{2,7},{3,6},{4,1},{5,0},{6,3},{7,2},{8,13},{9,12},{10,... | collective-permute-start | bytes 82952 | tf_op jit(solution)/shard_map/cond/branch_1_fun/ppermute | solution.py:848
  213.9 4.1 %collective-permute-start.16 = (f32[9,768]{1,0:T(8,128)S(1)}, f32[9,768]{1,0:T(8,128)S(1)}, u32[]{:S(2)}, u32[]{:S(2)}) collective-permute-start(f32[9,768]{1,0:T(8,128)S(1)} %bitcast.9), channel_id=1, source_target_pairs={{0,1},{1,0},{2,3},{3,2},{4,5},{5,4},{6,7},{7,6},{8,9},{9,8},{10,11... | collective-permute-start | bytes 82952 | tf_op jit(solution)/shard_map/cond/branch_1_fun/ppermute | solution.py:636
  213.9 4.6 %collective-permute-start.18 = (f32[12,768]{1,0:T(8,128)S(1)}, f32[12,768]{1,0:T(8,128)S(1)}, u32[]{:S(2)}, u32[]{:S(2)}) collective-permute-start(f32[12,768]{1,0:T(8,128)S(1)} %add.64), channel_id=1, source_target_pairs={{0,4},{2,6},{4,0},{6,2},{8,12},{10,14},{12,8},{14,10},{16,20},{18,... | collective-permute-start | bytes 110600 | tf_op jit(solution)/shard_map/cond/branch_1_fun/ppermute | solution.py:545
  214.6 4.0 %collective-permute-start.14 = (bf16[384,384]{1,0:T(8,128)(2,1)S(1)}, bf16[384,384]{1,0:T(8,128)(2,1)S(1)}, u32[]{:S(2)}, u32[]{:S(2)}) collective-permute-start(bf16[384,384]{1,0:T(8,128)(2,1)S(1)} %collective-permute-done.9.refs_4_), channel_id=1, source_target_pairs={{0,2},{2,0},{4,6},{6,4},{8,10},{10,8},{12,14},{14,12},{16,18},{18,... | collective-permute-start | bytes 884744 | tf_op jit(solution)/shard_map/cond/branch_1_fun/ppermute | solution.py:545
  214.6 9.8 %collective-permute-start.13 = (bf16[384,384]{1,0:T(8,128)(2,1)S(1)}, bf16[384,384]{1,0:T(8,128)(2,1)S(1)}, u32[]{:S(2)}, u32[]{:S(2)}) collective-permute-start(bf16[384,384]{1,0:T(8,128)(2,1)S(1)} %collective-permute-done.9.refs_4_), channel_id=1, source_target_pairs={{0,4},{2,6},{4,0},{6,2},{8,12},{10,14},{12,8},{14,10},{16,20},{18,... | collective-permute-start | bytes 884744 | tf_op jit(solution)/shard_map/cond/branch_1_fun/ppermute | solution.py:545
  216.0 2.5 %collective-permute-start.15 = (bf16[384,384]{1,0:T(8,128)(2,1)S(1)}, bf16[384,384]{1,0:T(8,128)(2,1)S(1)}, u32[]{:S(2)}, u32[]{:S(2)}) collective-permute-start(bf16[384,384]{1,0:T(8,128)(2,1)S(1)} %collective-permute-done.10.refs_2_), channel_id=1, source_target_pairs={{0,2},{2,0},{4,6},{6,4},{8,10},{10,8},{12,14},{14,12},{16,18},{18,... | collective-permute-start | bytes 884744 | tf_op jit(solution)/shard_map/cond/branch_1_fun/ppermute | solution.py:545
  224.4 1.7 collective-permute-start.20
  224.4 1.6 collective-permute-start.19
  (49 other events, 449.5 us)
Sparse Core Ops, SparseCore 0:
  85.3 137.6 all-reduce.2
